TPU v7x, 32 devices: a whole 2x2x4 slice. The times are simulated.
32 devices in a mesh: section: 4 (over z), dp: 4 (over x, core), tensor: 2 (over y).
Axes of the slice: x: 2, y: 2, z: 4, core: 2. Of those that a mesh axis runs over, the one named last changes fastest.
Arguments:
- activations: bfloat16 [4, 512, 4096], P('section', 'dp', 'tensor'), may hold values from -32 to 32
- norm_gain: float32 [4, 4096], P('section', 'tensor'), may hold values from 0.5 to 2
- weights: bfloat16 [4, 4096, 1024], P('section', 'tensor'), may hold values from -0.09375 to 0.09375
- cotangent: bfloat16 [4, 512, 1024], P('section', 'dp'), may hold values from -16 to 16
- top_grad: bfloat16 [512, 4096], P('dp', 'tensor'), may hold values from -6 to 6
- owner_slot: int32 [4, 2, 13], P('section', 'tensor'), may hold values from 0 to 15, as said below
- sweeps: int32 [4, 2, 4], P('section', 'tensor'), may hold values from 3 to 6
Outputs:
- input_grad: bfloat16 [4, 512, 4096], P('section', 'dp', 'tensor')
- preconditioned: bfloat16 [4, 4096, 1024], P('section', 'tensor')
Inputs may be any that keep to these rules, and one draw needn't show every extreme that they name: For each section and tensor index the 13 entries are distinct; the unit is owned by data replica owner_slot // 4, so a replica owns at most 4 units, and some replica owns exactly 4.
All inputs are finite; a program needn't handle non-finite values.
Results may differ from a plain program's by a relative error of at most 0.035.
Values may be sent and summed in bfloat16 or wider, within the bound.
No kernel may reach another device: no remote copies, remote signals or barrier semaphores. Data moves between devices by JAX's collectives and lax.ppermute only.
A program may use at most 128 MiB of HBM per device.

v0:
```python
import functools

import jax
import jax.numpy as jnp
from jax import lax
from jax.experimental import pallas as pl
from jax.experimental.pallas import tpu as pltpu
from jax.sharding import PartitionSpec as P


BLOCK = 512
EPSILON = 1e-05
DAMPING = 0.05
LANES = 128
STAT_ROWS = 8
RELAY_CHUNKS = 2
RELAY_LAG = 1
VMEM_LIMIT = 24 * 2**20


def flipped(value, axis, bit):
    count = lax.axis_size(axis)
    return lax.ppermute(value, axis, [(k, k ^ bit) for k in range(count)])


def higher_bits(axis):
    bit = 2
    while bit < lax.axis_size(axis):
        yield bit
        bit *= 2


def first_dim_product(left, right):
    return lax.dot_general(
        left, right, (((0,), (0,)), ((), ())), preferred_element_type=jnp.float32
    )


def product(left, right):
    return jnp.dot(left, right, preferred_element_type=jnp.float32)


def inverse_of(tokens, limit, state, halves):
    count, order = tokens.shape
    rows = lax.broadcasted_iota(jnp.int32, (order, order), 0)
    columns = lax.broadcasted_iota(jnp.int32, (order, order), 1)
    diagonal = rows == columns
    matrix = first_dim_product(tokens, tokens) * (1.0 / count)
    matrix = matrix + jnp.where(diagonal, DAMPING, 0.0)
    scale = lax.rsqrt(jnp.sum(matrix * matrix))
    first = matrix * scale
    start = jnp.where(diagonal, 2.0, 0.0) - first
    first_half = first.astype(jnp.bfloat16)
    state[0] = start
    halves[0:order] = start.astype(jnp.bfloat16)
    grown = 2.0 * first - product(first_half, first_half)
    state[1] = grown
    halves[order:] = grown.astype(jnp.bfloat16)

    def sweep(k, carry):
        change = product(halves[...], halves[order:])
        approx = 2.0 * state[0] - change[:order]
        grown = 2.0 * state[1] - change[order:]
        state[0] = approx
        state[1] = grown
        halves[0:order] = approx.astype(jnp.bfloat16)
        halves[order:] = grown.astype(jnp.bfloat16)
        return carry

    lax.fori_loop(2, limit, sweep, 0)
    last = 2.0 * state[0] - product(halves[0:order], halves[order:])
    return (last * scale).astype(jnp.bfloat16)


def upstream_kernel(
    table, counts, cot_hbm, weight_hbm, act_hbm, gain_hbm, scaled_ref, stats_ref, cot, weight, act, gain, sems, *, position, capacity
):
    tokens, width = act.shape
    blocks = width // BLOCK
    small = [
        pltpu.make_async_copy(source, target, sems.at[k])
        for k, (source, target) in enumerate(((act_hbm, act), (cot_hbm, cot), (gain_hbm, gain)))
    ]
    large = [
        pltpu.make_async_copy(
            weight_hbm.at[pl.ds(k * BLOCK, BLOCK)],
            weight.at[pl.ds(k * BLOCK, BLOCK)],
            sems.at[3 + k],
        )
        for k in range(blocks)
    ]
    for copy in small + large:
        copy.start()
    small[0].wait()
    squares = jnp.zeros((tokens, LANES), jnp.float32)
    for k in range(width // LANES):
        inputs = act[:, k * LANES : (k + 1) * LANES].astype(jnp.float32)
        squares += inputs * inputs
    limit = counts[table[position] // capacity].astype(jnp.float32)
    stats_ref[...] = jnp.full(stats_ref.shape, limit, jnp.float32)
    stats_ref[0:1] = jnp.sum(squares.T, axis=0, keepdims=True)
    small[1].wait()
    small[2].wait()
    inner = jnp.zeros((tokens, LANES), jnp.float32)
    for k in range(blocks):
        span = slice(k * BLOCK, (k + 1) * BLOCK)
        large[k].wait()
        upstream = lax.dot_general(
            cot[...], weight[span], (((1,), (1,)), ((), ())), preferred_element_type=jnp.float32
        )
        scaled = upstream * gain[:, span]
        scaled_ref[:, span] = scaled
        for j in range(BLOCK // LANES):
            lanes = slice(j * LANES, (j + 1) * LANES)
            start = k * BLOCK + j * LANES
            inner += scaled[:, lanes] * act[:, start : start + LANES].astype(jnp.float32)
    stats_ref[1:2] = jnp.sum(inner.T, axis=0, keepdims=True)


SMEM = pl.BlockSpec(memory_space=pltpu.SMEM)
VMEM = pl.BlockSpec(memory_space=pltpu.VMEM)
HBM = pl.BlockSpec(memory_space=pltpu.HBM)


def in_hbm(*arrays):
    return [pltpu.with_memory_space_constraint(array, pltpu.HBM) for array in arrays]


def in_vmem(*arrays):
    return [pltpu.with_memory_space_constraint(array, pltpu.VMEM) for array in arrays]


def upstream_of(table, counts, cotangent, weights, activations, gain, position, capacity):
    tokens, value_width = cotangent.shape
    width = weights.shape[0]
    return pl.pallas_call(
        functools.partial(upstream_kernel, position=position, capacity=capacity),
        in_specs=[SMEM, SMEM, HBM, HBM, HBM, HBM],
        out_specs=[VMEM, VMEM],
        out_shape=[
            jax.ShapeDtypeStruct((tokens, width), jnp.float32),
            jax.ShapeDtypeStruct((STAT_ROWS, tokens), jnp.float32),
        ],
        scratch_shapes=[
            pltpu.VMEM(cotangent.shape, cotangent.dtype),
            pltpu.VMEM(weights.shape, weights.dtype),
            pltpu.VMEM(activations.shape, activations.dtype),
            pltpu.VMEM(gain.shape, gain.dtype),
            pltpu.SemaphoreType.DMA((3 + width // BLOCK,)),
        ],
        compiler_params=pltpu.CompilerParams(vmem_limit_bytes=VMEM_LIMIT),
        cost_estimate=pl.CostEstimate(
            flops=2 * tokens * width * value_width,
            bytes_accessed=2 * width * value_width + 8 * tokens * width,
            transcendentals=0,
        ),
        name="upstream",
    )(*in_hbm(table, counts, cotangent, weights, activations, gain))


def column(row):
    return jnp.broadcast_to(row, (LANES, row.shape[1])).T[:, :1]


def terms_kernel(core, scaled_ref, act_ref, gain_ref, own_ref, other_ref, term_ref, *refs, full_width):
    normed, first_sent, pieces = refs[-1], refs[-2], refs[:-2]
    squares = own_ref[0:1] + other_ref[0:1]
    inner_sum = own_ref[1:2] + other_ref[1:2]
    inverse_rms = lax.rsqrt(squares * (1.0 / full_width) + EPSILON)
    coefficient = inverse_rms * inverse_rms * inverse_rms * inner_sum * (1.0 / full_width)
    inverse_rms, coefficient = column(inverse_rms), column(coefficient)
    inputs = act_ref[...].astype(jnp.float32)
    normed[...] = (inputs * inverse_rms * gain_ref[...]).astype(jnp.bfloat16)
    term = inverse_rms * scaled_ref[...] - inputs * coefficient
    term_ref[...] = term.astype(jnp.bfloat16)
    first_sent[...] = term[: first_sent.shape[0]].astype(jnp.bfloat16)
    half = normed.shape[1] // 2
    blocks = half // BLOCK
    for k in range(blocks):
        mine = pl.multiple_of(core[0] * half + k * BLOCK, BLOCK)
        theirs = pl.multiple_of((1 - core[0]) * half + k * BLOCK, BLOCK)
        pieces[k][...] = normed[:, pl.ds(mine, BLOCK)]
        pieces[blocks + k][...] = normed[:, pl.ds(theirs, BLOCK)]


def terms_of(core, scaled, activations, gain, own_stats, other_stats, full_width):
    tokens, width = scaled.shape
    blocks = width // BLOCK
    smem = pl.BlockSpec(memory_space=pltpu.SMEM)
    vmem = pl.BlockSpec(memory_space=pltpu.VMEM)
    outs = pl.pallas_call(
        functools.partial(terms_kernel, full_width=full_width),
        in_specs=[smem] + [vmem] * 5,
        out_specs=[vmem] * (2 + blocks),
        out_shape=[jax.ShapeDtypeStruct((tokens, width), jnp.bfloat16)]
        + [jax.ShapeDtypeStruct((tokens, BLOCK), jnp.bfloat16)] * blocks
        + [jax.ShapeDtypeStruct((tokens // RELAY_CHUNKS, width), jnp.bfloat16)],
        scratch_shapes=[pltpu.VMEM((tokens, width), jnp.bfloat16)],
        compiler_params=pltpu.CompilerParams(vmem_limit_bytes=VMEM_LIMIT),
        cost_estimate=pl.CostEstimate(
            flops=8 * tokens * width, bytes_accessed=10 * tokens * width, transcendentals=0
        ),
        name="terms",
    )(core, *in_vmem(scaled, activations, gain, own_stats, other_stats))
    return outs[0], outs[-1], outs[1 : 1 + blocks // 2], outs[1 + blocks // 2 : -1]


def relay(term, first_sent, axis):
    count, index = lax.axis_size(axis), lax.axis_index(axis)
    rows = term.shape[0] // RELAY_CHUNKS
    arrived = []
    for wave in range(RELAY_CHUNKS + RELAY_LAG * (count - 2)):
        chunk = jnp.clip(wave - RELAY_LAG * (count - 1 - index), 0, RELAY_CHUNKS - 1)
        sent = lax.dynamic_slice_in_dim(term, chunk * rows, rows, 0) if wave else first_sent
        if wave >= RELAY_LAG:
            before = arrived[wave - RELAY_LAG].astype(jnp.float32)
            sent = (sent.astype(jnp.float32) + before).astype(jnp.bfloat16)
        pairs = [(k, k - 1) for k in range(1, count)]
        arrived.append(lax.ppermute(sent, axis, pairs))
    return arrived


def finish_kernel(section, top_ref, term_ref, *refs, sections):
    arrived, out = refs[:-1], refs[-1]
    rows = arrived[0].shape[0]
    for chunk in range(RELAY_CHUNKS):
        span = slice(chunk * rows, (chunk + 1) * rows)
        own = top_ref[span].astype(jnp.float32) + term_ref[span].astype(jnp.float32)

        @pl.when(section[0] == sections - 1)
        def _(span=span, own=own):
            out[span] = own.astype(jnp.bfloat16)

        for place in range(sections - 1):
            later = arrived[chunk + RELAY_LAG * (sections - 2 - place)]

            @pl.when(section[0] == place)
            def _(span=span, own=own, later=later):
                out[span] = (own + later[...].astype(jnp.float32)).astype(jnp.bfloat16)


def finish(section, sections, top_grad, term, arrived):
    vmem = pl.BlockSpec(memory_space=pltpu.VMEM)
    return pl.pallas_call(
        functools.partial(finish_kernel, sections=sections),
        in_specs=[pl.BlockSpec(memory_space=pltpu.SMEM)] + [vmem] * (2 + len(arrived)),
        out_specs=vmem,
        out_shape=jax.ShapeDtypeStruct(term.shape, jnp.bfloat16),
        compiler_params=pltpu.CompilerParams(vmem_limit_bytes=VMEM_LIMIT),
        cost_estimate=pl.CostEstimate(
            flops=2 * term.size, bytes_accessed=8 * term.size, transcendentals=0
        ),
        name="finish",
    )(section, *in_vmem(top_grad, term, *arrived))


def scratch():
    return [
        pltpu.VMEM((2, BLOCK, BLOCK), jnp.float32),
        pltpu.VMEM((2 * BLOCK, BLOCK), jnp.bfloat16),
    ]


def row_copies(pieces, target, sems, first=0):
    rows = target.shape[0] // len(pieces)
    return [
        pltpu.make_async_copy(piece, target.at[pl.ds(k * rows, rows)], sems.at[first + k])
        for k, piece in enumerate(pieces)
    ]


def value_kernel(place, own_stats, other_stats, *refs, pieces):
    span = pl.ds(pl.multiple_of(place[0] * BLOCK, BLOCK), BLOCK)
    out, state, halves, tokens, sems = refs[pieces:]
    copies = row_copies([ref.at[:, span] for ref in refs[:pieces]], tokens, sems)
    for copy in copies:
        copy.start()
    for copy in copies:
        copy.wait()
    own_limit, other_limit = jnp.max(own_stats[2:3]), jnp.max(other_stats[2:3])
    limit = jnp.where(place[0] == place[1], own_limit, other_limit).astype(jnp.int32)
    out[...] = inverse_of(tokens[...], limit, state, halves)


def invert_value(place, own_stats, other_stats, pieces):
    return pl.pallas_call(
        functools.partial(value_kernel, pieces=len(pieces)),
        in_specs=[SMEM, VMEM, VMEM] + [HBM] * len(pieces),
        out_specs=VMEM,
        scratch_shapes=scratch()
        + [
            pltpu.VMEM((len(pieces) * pieces[0].shape[0], BLOCK), jnp.bfloat16),
            pltpu.SemaphoreType.DMA((len(pieces),)),
        ],
        out_shape=jax.ShapeDtypeStruct((BLOCK, BLOCK), jnp.bfloat16),
        compiler_params=pltpu.CompilerParams(vmem_limit_bytes=VMEM_LIMIT),
        cost_estimate=pl.CostEstimate(
            flops=22 * BLOCK**3, bytes_accessed=4 * BLOCK**2, transcendentals=0
        ),
        name="value_inverse",
    )(place, *in_vmem(own_stats, other_stats), *in_hbm(*pieces))


def feature_kernel(core, table, counts, *refs, pieces, place, half_blocks, capacity):
    own_inverse, other_inverse = refs[2 * pieces], refs[2 * pieces + 1]
    out, state, halves, left, normed, cotangent, sems = refs[-7:]
    copies = row_copies(refs[:pieces], normed, sems)
    later = row_copies(refs[pieces : 2 * pieces], cotangent, sems, pieces)
    for copy in copies + later:
        copy.start()
    for copy in copies:
        copy.wait()
    owner = table[core[0] * half_blocks + place] // capacity
    inverse = inverse_of(normed[...], counts[owner], state, halves)
    for copy in later:
        copy.wait()
    grad = first_dim_product(normed[...], cotangent[...]).astype(jnp.bfloat16)
    left[...] = product(inverse, grad).astype(jnp.bfloat16)
    for turn, value_inverse in ((0, own_inverse), (1, other_inverse)):
        block = core[0] if turn == 0 else 1 - core[0]
        span = pl.ds(pl.multiple_of(block * BLOCK, BLOCK), BLOCK)
        out[:, span] = product(left[:, span], value_inverse[...]).astype(jnp.bfloat16)


def precondition(core, table, counts, normed, cotangents, inverses, place, half_blocks, capacity):
    value_width = cotangents[0].shape[1]
    pieces = len(normed)
    tokens = pieces * normed[0].shape[0]
    return pl.pallas_call(
        functools.partial(
            feature_kernel, pieces=pieces, place=place, half_blocks=half_blocks, capacity=capacity
        ),
        in_specs=[SMEM] * 3 + [HBM] * (2 * pieces) + [VMEM] * 2,
        out_specs=VMEM,
        scratch_shapes=scratch()
        + [
            pltpu.VMEM((BLOCK, value_width), jnp.bfloat16),
            pltpu.VMEM((tokens, BLOCK), jnp.bfloat16),
            pltpu.VMEM((tokens, value_width), jnp.bfloat16),
            pltpu.SemaphoreType.DMA((2 * pieces,)),
        ],
        out_shape=jax.ShapeDtypeStruct((BLOCK, value_width), jnp.bfloat16),
        compiler_params=pltpu.CompilerParams(vmem_limit_bytes=VMEM_LIMIT),
        cost_estimate=pl.CostEstimate(
            flops=34 * BLOCK**3, bytes_accessed=8 * BLOCK**2, transcendentals=0
        ),
        name="precondition",
    )(core, *in_hbm(table, counts, *normed, *cotangents), *in_vmem(*inverses))


def place_kernel(core, *refs, blocks):
    pieces, out, sems = refs[: 2 * blocks], refs[-2], refs[-1]
    copies = []
    for k, piece in enumerate(pieces):
        owner = core[0] if k < blocks else 1 - core[0]
        start = pl.multiple_of((owner * blocks + k % blocks) * BLOCK, BLOCK)
        copies.append(pltpu.make_async_copy(piece, out.at[pl.ds(start, BLOCK)], sems.at[k]))
    for copy in copies:
        copy.start()
    for copy in copies:
        copy.wait()


def place_rows(core, own, received):
    blocks = len(received)
    value_width = received[0].shape[1]
    return pl.pallas_call(
        functools.partial(place_kernel, blocks=blocks),
        in_specs=[SMEM] + [VMEM] * (2 * blocks),
        out_specs=HBM,
        out_shape=jax.ShapeDtypeStruct((2 * blocks * BLOCK, value_width), jnp.bfloat16),
        scratch_shapes=[pltpu.SemaphoreType.DMA((2 * blocks,))],
        compiler_params=pltpu.CompilerParams(vmem_limit_bytes=VMEM_LIMIT),
        cost_estimate=pl.CostEstimate(
            flops=0, bytes_accessed=8 * blocks * BLOCK * value_width, transcendentals=0
        ),
        name="place_rows",
    )(core, *in_vmem(*own, *received))


def placed_work(activations, norm_gain, weights, cotangent, top_grad, owner_slot, sweeps):
    acts, cot = activations[0], cotangent[0]
    table, counts = owner_slot[0, 0], sweeps[0, 0]
    _, half_width = acts.shape
    value_width = cot.shape[1]
    tensor_size = lax.axis_size("tensor")
    replica_count = lax.axis_size("dp")
    feature_blocks = half_width // BLOCK
    value_blocks = value_width // BLOCK
    unit_count = feature_blocks + 1 + feature_blocks * value_blocks
    capacity = (unit_count + replica_count - 1) // replica_count
    half_blocks = feature_blocks // 2
    core = (lax.axis_index("dp") % 2)[None]

    far = [cot]
    for bit in higher_bits("dp"):
        far = far + [flipped(piece, "dp", bit) for piece in far]
    cotangents = []
    for piece in far:
        cotangents += [piece, flipped(piece, "dp", 1)]

    scaled, own_stats = upstream_of(
        table, counts, cot, weights[0], acts, norm_gain, feature_blocks, capacity
    )
    other_stats = flipped(own_stats, "tensor", 1)
    term, first_sent, mine, theirs = terms_of(
        core, scaled, acts, norm_gain, own_stats, other_stats, half_width * tensor_size
    )
    arrived = relay(term, first_sent, "section")

    normed = []
    for own, sent in zip(mine, theirs):
        pieces = [own]
        for mask in range(1, replica_count):
            pieces.append(flipped(sent if mask % 2 else own, "dp", mask))
        normed.append(pieces)

    place = jnp.stack([core[0], lax.axis_index("tensor")])
    own_inverse = invert_value(place, own_stats, other_stats, cotangents)
    inverses = [own_inverse, flipped(own_inverse, "dp", 1)]

    own_rows, received = [], []
    for k in range(half_blocks):
        own_rows.append(
            precondition(
                core, table, counts, normed[k], cotangents, inverses, k, half_blocks, capacity
            )
        )
        received.append(flipped(own_rows[k], "dp", 1))
    output = place_rows(core, own_rows, received)
    section = lax.axis_index("section")[None]
    input_grad = finish(section, lax.axis_size("section"), top_grad, term, arrived)
    return (input_grad[None], output[None])


def solution(mesh):
    placed = (
        P("section", "dp", "tensor"),
        P("section", "tensor"),
        P("section", "tensor", None),
        P("section", "dp", None),
        P("dp", "tensor"),
        P("section", "tensor", None),
        P("section", "tensor", None),
    )
    return jax.shard_map(
        placed_work,
        mesh=mesh,
        in_specs=placed,
        out_specs=(P("section", "dp", "tensor"), P("section", "tensor", None)),
        check_vma=False,
    )
```

profile of v0, /device:TPU:0, one launch (start us, length us, event | category | flops | bytes accessed | tf_op | source)
XLA Modules:
  0.0 88.5 jit_solution(14133640697022355052)
XLA Ops:
  0.6 3.0 %collective-permute-start.9 = (bf16[128,1024]{1,0:T(8,128)(2,1)}, bf16[128,1024]{1,0:T(8,128)(2,1)S(1)}, u32[]{:S(2)}, u32[]{:S(2)}) collective-permute-start(bf16[128,1024]{1,0:T(8,128)(2,1)} %bitcast.15), channel_id=1, source_target_pairs={{0,4},{2,6},{4,0},{6,2},{1,5},{3,7},{5,1},{7,3},{8,12},{10,14},{12... | collective-permute-start | bytes 786440 | tf_op jit(solution)/shard_map/ppermute | solution.py:23
  3.7 6.5 %collective-permute-done.9.refs_2_.refs_6_ = bf16[128,1024]{1,0:T(8,128)(2,1)S(1)} collective-permute-done((bf16[128,1024]{1,0:T(8,128)(2,1)}, bf16[128,1024]{1,0:T(8,128)(2,1)S(1)}, u32[]{:S(2)}, u32[]{:S(2)}) %collective-permute-start.9) | collective-permute-done | bytes 262176 | tf_op jit(solution)/shard_map/ppermute | solution.py:23
  10.2 4.2 %upstream.1 = (f32[128,2048]{1,0:T(8,128)S(1)}, f32[8,128]{1,0:T(8,128)S(1)}) custom-call(s32[13]{0:T(128)} %bitcast.21, s32[4]{0:T(128)} %bitcast.24, bf16[128,1024]{1,0:T(8,128)(2,1)} %bitcast.17, bf16[2048,1024]{1,0:T(8,128)(2,1)} %bitcast.12, bf16[128,2048]{1,0:T(8,128)(2,1)} %bitcast.10, f32[1,2048]{1,0:T(1,128)} %gain_ref.1), custom_call_target="tpu_custom_call" | custom-call | flops 536870912 | bytes 6291456 | tf_op jit(solution)/shard_map/upstream/pallas_call | solution.py:136
  14.5 1.8 %collective-permute-start = (f32[8,128]{1,0:T(8,128)S(1)}, f32[8,128]{1,0:T(8,128)S(1)}, u32[]{:S(2)}, u32[]{:S(2)}) collective-permute-start(f32[8,128]{1,0:T(8,128)S(1)} %get-tuple-element.11.own_ref.own_stats), channel_id=1, source_target_pairs={{0,1},{1,0},{2,3},{3,2},{4,5},{5,4},{6,7},{7,6},{8,9},{9,8},{10,11... | collective-permute-start | bytes 12296 | tf_op jit(solution)/shard_map/ppermute | solution.py:23
  16.4 1.8 %collective-permute-done.other_ref.other_stats = f32[8,128]{1,0:T(8,128)S(1)} collective-permute-done((f32[8,128]{1,0:T(8,128)S(1)}, f32[8,128]{1,0:T(8,128)S(1)}, u32[]{:S(2)}, u32[]{:S(2)}) %collective-permute-start) | collective-permute-done | bytes 4128 | tf_op jit(solution)/shard_map/ppermute | solution.py:23
  18.1 0.4 terms.1
  18.6 0.6 copy-done.9
  19.2 1.4 %collective-permute-start.1 = (bf16[64,2048]{1,0:T(8,128)(2,1)S(1)}, bf16[64,2048]{1,0:T(8,128)(2,1)S(1)}, u32[]{:S(2)}, u32[]{:S(2)}) collective-permute-start(bf16[64,2048]{1,0:T(8,128)(2,1)S(1)} %get-tuple-element.13), channel_id=1, source_target_pairs={{8,0},{16,8},{24,16},{9,1},{17,9},{25,17},{10,2},{18,10},{26,18},{... | collective-permute-start | bytes 786440 | tf_op jit(solution)/shard_map/ppermute | solution.py:219
  20.7 6.4 %value_inverse.1.refs_8_ = bf16[512,512]{1,0:T(8,128)(2,1)S(1)} custom-call(s32[2]{0:T(128)S(1)} %pad_add_fusion.place, f32[8,128]{1,0:T(8,128)S(1)} %get-tuple-element.11.own_ref.own_stats, f32[8,128]{1,0:T(8,128)S(1)} %collective-permute-done.other_ref.other_stats, bf16[128,1024]{1,0:T(8,128)(2,1)} %bitcast.18, ...), custom_call_target="tpu_custom_call" | custom-call | flops 2952790016 | bytes 1048576 | tf_op jit(solution)/shard_map/value_inverse/pallas_call | solution.py:286
  27.2 1.8 %collective-permute-start.7 = (bf16[128,512]{1,0:T(8,128)(2,1)S(1)}, bf16[128,512]{1,0:T(8,128)(2,1)S(1)}, u32[]{:S(2)}, u32[]{:S(2)}) collective-permute-start(bf16[128,512]{1,0:T(8,128)(2,1)S(1)} %copy-done.10), channel_id=1, source_target_pairs={{0,6},{2,4},{4,2},{6,0},{1,7},{3,5},{5,3},{7,1},{8,14},{10,12},{12... | collective-permute-start | bytes 393224 | tf_op jit(solution)/shard_map/ppermute | solution.py:23
  29.0 0.1 collective-permute-start.5
  29.1 0.3 collective-permute-start.6
  29.4 1.5 %collective-permute-start.14 = (bf16[128,512]{1,0:T(8,128)(2,1)S(1)}, bf16[128,512]{1,0:T(8,128)(2,1)S(1)}, u32[]{:S(2)}, u32[]{:S(2)}) collective-permute-start(bf16[128,512]{1,0:T(8,128)(2,1)S(1)} %get-tuple-element.17), channel_id=1, source_target_pairs={{0,6},{2,4},{4,2},{6,0},{1,7},{3,5},{5,3},{7,1},{8,14},{10,12},{12... | collective-permute-start | bytes 393224 | tf_op jit(solution)/shard_map/ppermute | solution.py:23
  30.9 5.5 %collective-permute-done.6.refs_2_ = bf16[128,512]{1,0:T(8,128)(2,1)S(1)} collective-permute-done((bf16[128,512]{1,0:T(8,128)(2,1)S(1)}, bf16[128,512]{1,0:T(8,128)(2,1)S(1)}, u32[]{:S(2)}, u32[]{:S(2)}) %collective-permute-start.6) | collective-permute-done | bytes 131104 | tf_op jit(solution)/shard_map/ppermute | solution.py:23
  36.5 1.8 %collective-permute-start.13 = (bf16[128,512]{1,0:T(8,128)(2,1)S(1)}, bf16[128,512]{1,0:T(8,128)(2,1)S(1)}, u32[]{:S(2)}, u32[]{:S(2)}) collective-permute-start(bf16[128,512]{1,0:T(8,128)(2,1)S(1)} %get-tuple-element.16.refs_0_), channel_id=1, source_target_pairs={{0,4},{2,6},{4,0},{6,2},{1,5},{3,7},{5,1},{7,3},{8,12},{10,14},{12... | collective-permute-start | bytes 393224 | tf_op jit(solution)/shard_map/ppermute | solution.py:23
  38.3 1.3 %collective-permute-start.2 = (bf16[64,2048]{1,0:T(8,128)(2,1)S(1)}, bf16[64,2048]{1,0:T(8,128)(2,1)S(1)}, u32[]{:S(2)}, u32[]{:S(2)}) collective-permute-start(bf16[64,2048]{1,0:T(8,128)(2,1)S(1)} %add_convert_fusion.2), channel_id=1, source_target_pairs={{8,0},{16,8},{24,16},{9,1},{17,9},{25,17},{10,2},{18,10},{26,18},{... | collective-permute-start | bytes 786440 | tf_op jit(solution)/shard_map/ppermute | solution.py:219
  39.6 6.4 %precondition.2.refs_0_ = bf16[512,1024]{1,0:T(8,128)(2,1)S(1)} custom-call(s32[1]{0:T(128)} %bitcast.1.core, s32[13]{0:T(128)} %bitcast.22, s32[4]{0:T(128)} %bitcast.25, bf16[128,512]{1,0:T(8,128)(2,1)} %copy-done.8, bf16[128,512]{1,0:T(8,128)(2,1)} %copy-done.15, bf16[128,512]{1,0:T(8,128)(2,1)} %copy-done.16, bf16[128,512]{1,0:T(8,128)(2,1)} %copy-done.13, ...), custom_call_target="tpu_custom_call" | custom-call | flops 4563402752 | bytes 2097152 | tf_op jit(solution)/shard_map/precondition/pallas_call | solution.py:329
  46.0 0.8 copy-done.5
  46.8 2.3 %collective-permute-start.15 = (bf16[512,1024]{1,0:T(8,128)(2,1)S(1)}, bf16[512,1024]{1,0:T(8,128)(2,1)S(1)}, u32[]{:S(2)}, u32[]{:S(2)}) collective-permute-start(bf16[512,1024]{1,0:T(8,128)(2,1)S(1)} %precondition.2.refs_0_), channel_id=1, source_target_pairs={{0,2},{2,0},{4,6},{6,4},{1,3},{3,1},{5,7},{7,5},{8,10},{10,8},{12,... | collective-permute-start | bytes 3145736 | tf_op jit(solution)/shard_map/ppermute | solution.py:23
  49.2 0.6 copy-done.17
  49.8 0.6 copy-done.14
  50.5 1.0 %copy-done.4 = bf16[512,512]{1,0:T(8,128)(2,1)S(1)} copy-done((bf16[512,512]{1,0:T(8,128)(2,1)S(1)}, bf16[512,512]{1,0:T(8,128)(2,1)}, u32[]{:S(2)}) %copy-start.4) | copy-done | bytes 524312
  51.5 1.0 %copy-done.6 = bf16[512,512]{1,0:T(8,128)(2,1)S(1)} copy-done((bf16[512,512]{1,0:T(8,128)(2,1)S(1)}, bf16[512,512]{1,0:T(8,128)(2,1)}, u32[]{:S(2)}) %copy-start.6) | copy-done | bytes 524312
  52.6 8.8 %precondition.3.refs_1_ = bf16[512,1024]{1,0:T(8,128)(2,1)} custom-call(s32[1]{0:T(128)} %bitcast.1.core, s32[13]{0:T(128)} %bitcast.23, s32[4]{0:T(128)} %bitcast.26, bf16[128,512]{1,0:T(8,128)(2,1)} %copy-done.7, bf16[128,512]{1,0:T(8,128)(2,1)} %copy-done.14, bf16[128,512]{1,0:T(8,128)(2,1)} %copy-done.17, bf16[128,512]{1,0:T(8,128)(2,1)} %copy-done.12, ...), custom_call_target="tpu_custom_call" | custom-call | flops 4563402752 | bytes 2097152 | tf_op jit(solution)/shard_map/precondition/pallas_call | solution.py:329
  61.4 0.8 add_convert_fusion.1
  62.2 1.3 %collective-permute-start.3 = (bf16[64,2048]{1,0:T(8,128)(2,1)}, bf16[64,2048]{1,0:T(8,128)(2,1)S(1)}, u32[]{:S(2)}, u32[]{:S(2)}) collective-permute-start(bf16[64,2048]{1,0:T(8,128)(2,1)} %add_convert_fusion.1), channel_id=1, source_target_pairs={{8,0},{16,8},{24,16},{9,1},{17,9},{25,17},{10,2},{18,10},{26,18},{... | collective-permute-start | bytes 786440 | tf_op jit(solution)/shard_map/ppermute | solution.py:219
  63.5 9.5 %collective-permute-done.3.refs_2_ = bf16[64,2048]{1,0:T(8,128)(2,1)S(1)} collective-permute-done((bf16[64,2048]{1,0:T(8,128)(2,1)}, bf16[64,2048]{1,0:T(8,128)(2,1)S(1)}, u32[]{:S(2)}, u32[]{:S(2)}) %collective-permute-start.3) | collective-permute-done | bytes 262176 | tf_op jit(solution)/shard_map/ppermute | solution.py:219
  73.1 1.3 %collective-permute-start.4 = (bf16[64,2048]{1,0:T(8,128)(2,1)S(1)}, bf16[64,2048]{1,0:T(8,128)(2,1)S(1)}, u32[]{:S(2)}, u32[]{:S(2)}) collective-permute-start(bf16[64,2048]{1,0:T(8,128)(2,1)S(1)} %add_convert_fusion), channel_id=1, source_target_pairs={{8,0},{16,8},{24,16},{9,1},{17,9},{25,17},{10,2},{18,10},{26,18},{... | collective-permute-start | bytes 786440 | tf_op jit(solution)/shard_map/ppermute | solution.py:219
  74.4 8.4 %collective-permute-done.4.refs_3_ = bf16[64,2048]{1,0:T(8,128)(2,1)S(1)} collective-permute-done((bf16[64,2048]{1,0:T(8,128)(2,1)S(1)}, bf16[64,2048]{1,0:T(8,128)(2,1)S(1)}, u32[]{:S(2)}, u32[]{:S(2)}) %collective-permute-start.4) | collective-permute-done | bytes 262176 | tf_op jit(solution)/shard_map/ppermute | solution.py:219
  82.8 1.0 %copy-done.1 = bf16[128,2048]{1,0:T(8,128)(2,1)S(1)} copy-done((bf16[128,2048]{1,0:T(8,128)(2,1)S(1)}, bf16[128,2048]{1,0:T(8,128)(2,1)}, u32[]{:S(2)}) %copy-start.1) | copy-done | bytes 524312
  83.8 1.1 %finish.1 = bf16[128,2048]{1,0:T(8,128)(2,1)} custom-call(s32[1]{0:T(128)} %bitcast.section, bf16[128,2048]{1,0:T(8,128)(2,1)S(1)} %copy-done.1, bf16[128,2048]{1,0:T(8,128)(2,1)S(1)} %get-tuple-element.12.term_ref, bf16[64,2048]{1,0:T(8,128)(2,1)S(1)} %collective-permute-done.1.refs_0_, bf16[64,2048]{1,0:T(8,128)(2,1)S(1)} %collective-permute-done.2.refs_1_, ...), custom_call_target="tpu_custom_call" | custom-call | flops 524288 | bytes 2097152 | tf_op jit(solution)/shard_map/finish/pallas_call | solution.py:244
  85.0 3.6 %place_rows.1 = bf16[2048,1024]{1,0:T(8,128)(2,1)} custom-call(s32[1]{0:T(128)} %bitcast.1.core, bf16[512,1024]{1,0:T(8,128)(2,1)S(1)} %precondition.2.refs_0_, bf16[512,1024]{1,0:T(8,128)(2,1)} %precondition.3.refs_1_, bf16[512,1024]{1,0:T(8,128)(2,1)S(1)} %collective-permute-done.15.refs_2_, bf16[512,1024]{1,0:T(8,128)(2,1)} %collective-permute-done.16.refs_3_), custom_call_target="tpu_custom_call" | custom-call | bytes 8388608 | tf_op jit(solution)/shard_map/place_rows/pallas_call | solution.py:367
  (49 shorter events, 0.5 us)
Async XLA Ops:
  0.6 17.5 %copy-start.2 = (f32[1,2048]{1,0:T(1,128)S(1)}, f32[1,2048]{1,0:T(1,128)}, u32[]{:S(2)}) copy-start(f32[1,2048]{1,0:T(1,128)} %gain_ref.1) | copy-start | bytes 24580
  0.6 17.5 %copy-start = (bf16[1,128,2048]{2,1,0:T(8,128)(2,1)S(1)}, bf16[1,128,2048]{2,1,0:T(8,128)(2,1)}, u32[]{:S(2)}) copy-start(bf16[1,128,2048]{2,1,0:T(8,128)(2,1)} %param.7) | copy-start | bytes 1572868
  0.6 9.6 %collective-permute-start.9 = (bf16[128,1024]{1,0:T(8,128)(2,1)}, bf16[128,1024]{1,0:T(8,128)(2,1)S(1)}, u32[]{:S(2)}, u32[]{:S(2)}) collective-permute-start(bf16[128,1024]{1,0:T(8,128)(2,1)} %bitcast.15), channel_id=1, source_target_pairs={{0,4},{2,6},{4,0},{6,2},{1,5},{3,7},{5,1},{7,3},{8,12},{10,14},{12... | collective-permute-start | bytes 786440 | tf_op jit(solution)/shard_map/ppermute | solution.py:23
  3.7 17.0 %collective-permute-start.8 = (bf16[128,1024]{1,0:T(8,128)(2,1)}, bf16[128,1024]{1,0:T(8,128)(2,1)}, u32[]{:S(2)}, u32[]{:S(2)}) collective-permute-start(bf16[128,1024]{1,0:T(8,128)(2,1)} %bitcast.16), channel_id=1, source_target_pairs={{0,2},{2,0},{4,6},{6,4},{1,3},{3,1},{5,7},{7,5},{8,10},{10,8},{12,... | collective-permute-start | bytes 786440 | tf_op jit(solution)/shard_map/ppermute | solution.py:23
  10.2 10.5 %copy-start.11 = (bf16[128,1024]{1,0:T(8,128)(2,1)}, bf16[128,1024]{1,0:T(8,128)(2,1)S(1)}, u32[]{:S(2)}) copy-start(bf16[128,1024]{1,0:T(8,128)(2,1)S(1)} %collective-permute-done.9.refs_2_.refs_6_) | copy-start | bytes 786436
  10.2 10.5 %collective-permute-start.10 = (bf16[128,1024]{1,0:T(8,128)(2,1)S(1)}, bf16[128,1024]{1,0:T(8,128)(2,1)}, u32[]{:S(2)}, u32[]{:S(2)}) collective-permute-start(bf16[128,1024]{1,0:T(8,128)(2,1)S(1)} %collective-permute-done.9.refs_2_.refs_6_), channel_id=1, source_target_pairs={{0,2},{2,0},{4,6},{6,4},{1,3},{3,1},{5,7},{7,5},{8,10},{10,8},{12,... | collective-permute-start | bytes 786440 | tf_op jit(solution)/shard_map/ppermute | solution.py:23
  14.5 3.7 %collective-permute-start = (f32[8,128]{1,0:T(8,128)S(1)}, f32[8,128]{1,0:T(8,128)S(1)}, u32[]{:S(2)}, u32[]{:S(2)}) collective-permute-start(f32[8,128]{1,0:T(8,128)S(1)} %get-tuple-element.11.own_ref.own_stats), channel_id=1, source_target_pairs={{0,1},{1,0},{2,3},{3,2},{4,5},{5,4},{6,7},{7,6},{8,9},{9,8},{10,11... | collective-permute-start | bytes 12296 | tf_op jit(solution)/shard_map/ppermute | solution.py:23
  19.2 9.9 %copy-start.8 = (bf16[128,512]{1,0:T(8,128)(2,1)}, bf16[128,512]{1,0:T(8,128)(2,1)S(1)}, u32[]{:S(2)}) copy-start(bf16[128,512]{1,0:T(8,128)(2,1)S(1)} %get-tuple-element.14.refs_0_) | copy-start | bytes 393220
  19.2 17.2 %copy-start.7 = (bf16[128,512]{1,0:T(8,128)(2,1)}, bf16[128,512]{1,0:T(8,128)(2,1)S(1)}, u32[]{:S(2)}) copy-start(bf16[128,512]{1,0:T(8,128)(2,1)S(1)} %get-tuple-element.16.refs_0_) | copy-start | bytes 393220
  19.2 7.9 %copy-start.10 = (bf16[128,512]{1,0:T(8,128)(2,1)S(1)}, bf16[128,512]{1,0:T(8,128)(2,1)}, u32[]{:S(2)}) copy-start(bf16[128,512]{1,0:T(8,128)(2,1)} %copy-done.9) | copy-start | bytes 393220
  19.2 10.2 %collective-permute-start.1 = (bf16[64,2048]{1,0:T(8,128)(2,1)S(1)}, bf16[64,2048]{1,0:T(8,128)(2,1)S(1)}, u32[]{:S(2)}, u32[]{:S(2)}) collective-permute-start(bf16[64,2048]{1,0:T(8,128)(2,1)S(1)} %get-tuple-element.13), channel_id=1, source_target_pairs={{8,0},{16,8},{24,16},{9,1},{17,9},{25,17},{10,2},{18,10},{26,18},{... | collective-permute-start | bytes 786440 | tf_op jit(solution)/shard_map/ppermute | solution.py:219
  27.1 12.5 %copy-start.3 = (bf16[512,512]{1,0:T(8,128)(2,1)}, bf16[512,512]{1,0:T(8,128)(2,1)S(1)}, u32[]{:S(2)}) copy-start(bf16[512,512]{1,0:T(8,128)(2,1)S(1)} %value_inverse.1.refs_8_) | copy-start | bytes 1572868
  27.1 12.5 %collective-permute-start.11 = (bf16[512,512]{1,0:T(8,128)(2,1)S(1)}, bf16[512,512]{1,0:T(8,128)(2,1)S(1)}, u32[]{:S(2)}, u32[]{:S(2)}) collective-permute-start(bf16[512,512]{1,0:T(8,128)(2,1)S(1)} %value_inverse.1.refs_8_), channel_id=1, source_target_pairs={{0,2},{2,0},{4,6},{6,4},{1,3},{3,1},{5,7},{7,5},{8,10},{10,8},{12,... | collective-permute-start | bytes 1572872 | tf_op jit(solution)/shard_map/ppermute | solution.py:23
  27.2 9.3 %collective-permute-start.7 = (bf16[128,512]{1,0:T(8,128)(2,1)S(1)}, bf16[128,512]{1,0:T(8,128)(2,1)S(1)}, u32[]{:S(2)}, u32[]{:S(2)}) collective-permute-start(bf16[128,512]{1,0:T(8,128)(2,1)S(1)} %copy-done.10), channel_id=1, source_target_pairs={{0,6},{2,4},{4,2},{6,0},{1,7},{3,5},{5,3},{7,1},{8,14},{10,12},{12... | collective-permute-start | bytes 393224 | tf_op jit(solution)/shard_map/ppermute | solution.py:23
  29.0 9.3 %collective-permute-start.5 = (bf16[128,512]{1,0:T(8,128)(2,1)S(1)}, bf16[128,512]{1,0:T(8,128)(2,1)S(1)}, u32[]{:S(2)}, u32[]{:S(2)}) collective-permute-start(bf16[128,512]{1,0:T(8,128)(2,1)S(1)} %copy-done.10), channel_id=1, source_target_pairs={{0,2},{2,0},{4,6},{6,4},{1,3},{3,1},{5,7},{7,5},{8,10},{10,8},{12,... | collective-permute-start | bytes 393224 | tf_op jit(solution)/shard_map/ppermute | solution.py:23
  29.1 7.3 %collective-permute-start.6 = (bf16[128,512]{1,0:T(8,128)(2,1)S(1)}, bf16[128,512]{1,0:T(8,128)(2,1)S(1)}, u32[]{:S(2)}, u32[]{:S(2)}) collective-permute-start(bf16[128,512]{1,0:T(8,128)(2,1)S(1)} %get-tuple-element.14.refs_0_), channel_id=1, source_target_pairs={{0,4},{2,6},{4,0},{6,2},{1,5},{3,7},{5,1},{7,3},{8,12},{10,14},{12... | collective-permute-start | bytes 393224 | tf_op jit(solution)/shard_map/ppermute | solution.py:23
  29.4 19.7 %collective-permute-start.14 = (bf16[128,512]{1,0:T(8,128)(2,1)S(1)}, bf16[128,512]{1,0:T(8,128)(2,1)S(1)}, u32[]{:S(2)}, u32[]{:S(2)}) collective-permute-start(bf16[128,512]{1,0:T(8,128)(2,1)S(1)} %get-tuple-element.17), channel_id=1, source_target_pairs={{0,6},{2,4},{4,2},{6,0},{1,7},{3,5},{5,3},{7,1},{8,14},{10,12},{12... | collective-permute-start | bytes 393224 | tf_op jit(solution)/shard_map/ppermute | solution.py:23
  36.4 3.2 %copy-start.16 = (bf16[128,512]{1,0:T(8,128)(2,1)}, bf16[128,512]{1,0:T(8,128)(2,1)S(1)}, u32[]{:S(2)}) copy-start(bf16[128,512]{1,0:T(8,128)(2,1)S(1)} %collective-permute-done.6.refs_2_) | copy-start | bytes 393220
  36.4 12.7 %collective-permute-start.12 = (bf16[128,512]{1,0:T(8,128)(2,1)S(1)}, bf16[128,512]{1,0:T(8,128)(2,1)S(1)}, u32[]{:S(2)}, u32[]{:S(2)}) collective-permute-start(bf16[128,512]{1,0:T(8,128)(2,1)S(1)} %get-tuple-element.17), channel_id=1, source_target_pairs={{0,2},{2,0},{4,6},{6,4},{1,3},{3,1},{5,7},{7,5},{8,10},{10,8},{12,... | collective-permute-start | bytes 393224 | tf_op jit(solution)/shard_map/ppermute | solution.py:23
  36.4 3.2 %copy-start.13 = (bf16[128,512]{1,0:T(8,128)(2,1)}, bf16[128,512]{1,0:T(8,128)(2,1)S(1)}, u32[]{:S(2)}) copy-start(bf16[128,512]{1,0:T(8,128)(2,1)S(1)} %collective-permute-done.7.refs_3_) | copy-start | bytes 393220
  36.5 12.7 %collective-permute-start.13 = (bf16[128,512]{1,0:T(8,128)(2,1)S(1)}, bf16[128,512]{1,0:T(8,128)(2,1)S(1)}, u32[]{:S(2)}, u32[]{:S(2)}) collective-permute-start(bf16[128,512]{1,0:T(8,128)(2,1)S(1)} %get-tuple-element.16.refs_0_), channel_id=1, source_target_pairs={{0,4},{2,6},{4,0},{6,2},{1,5},{3,7},{5,1},{7,3},{8,12},{10,14},{12... | collective-permute-start | bytes 393224 | tf_op jit(solution)/shard_map/ppermute | solution.py:23
  38.3 1.3 %copy-start.15 = (bf16[128,512]{1,0:T(8,128)(2,1)}, bf16[128,512]{1,0:T(8,128)(2,1)S(1)}, u32[]{:S(2)}) copy-start(bf16[128,512]{1,0:T(8,128)(2,1)S(1)} %collective-permute-done.5.refs_1_) | copy-start | bytes 393220
  38.3 23.2 %collective-permute-start.2 = (bf16[64,2048]{1,0:T(8,128)(2,1)S(1)}, bf16[64,2048]{1,0:T(8,128)(2,1)S(1)}, u32[]{:S(2)}, u32[]{:S(2)}) collective-permute-start(bf16[64,2048]{1,0:T(8,128)(2,1)S(1)} %add_convert_fusion.2), channel_id=1, source_target_pairs={{8,0},{16,8},{24,16},{9,1},{17,9},{25,17},{10,2},{18,10},{26,18},{... | collective-permute-start | bytes 786440 | tf_op jit(solution)/shard_map/ppermute | solution.py:219
  46.0 0.8 copy-start.5
  46.8 38.2 %collective-permute-start.15 = (bf16[512,1024]{1,0:T(8,128)(2,1)S(1)}, bf16[512,1024]{1,0:T(8,128)(2,1)S(1)}, u32[]{:S(2)}, u32[]{:S(2)}) collective-permute-start(bf16[512,1024]{1,0:T(8,128)(2,1)S(1)} %precondition.2.refs_0_), channel_id=1, source_target_pairs={{0,2},{2,0},{4,6},{6,4},{1,3},{3,1},{5,7},{7,5},{8,10},{10,8},{12,... | collective-permute-start | bytes 3145736 | tf_op jit(solution)/shard_map/ppermute | solution.py:23
  49.1 0.7 copy-start.12
  50.5 1.0 %copy-start.4 = (bf16[512,512]{1,0:T(8,128)(2,1)S(1)}, bf16[512,512]{1,0:T(8,128)(2,1)}, u32[]{:S(2)}) copy-start(bf16[512,512]{1,0:T(8,128)(2,1)} %copy-done.3) | copy-start | bytes 1572868
  51.5 1.0 %copy-start.6 = (bf16[512,512]{1,0:T(8,128)(2,1)S(1)}, bf16[512,512]{1,0:T(8,128)(2,1)}, u32[]{:S(2)}) copy-start(bf16[512,512]{1,0:T(8,128)(2,1)} %copy-done.5) | copy-start | bytes 1572868
  61.3 23.6 %collective-permute-start.16 = (bf16[512,1024]{1,0:T(8,128)(2,1)}, bf16[512,1024]{1,0:T(8,128)(2,1)}, u32[]{:S(2)}, u32[]{:S(2)}) collective-permute-start(bf16[512,1024]{1,0:T(8,128)(2,1)} %precondition.3.refs_1_), channel_id=1, source_target_pairs={{0,2},{2,0},{4,6},{6,4},{1,3},{3,1},{5,7},{7,5},{8,10},{10,8},{12,... | collective-permute-start | bytes 3145736 | tf_op jit(solution)/shard_map/ppermute | solution.py:23
  62.2 10.8 %collective-permute-start.3 = (bf16[64,2048]{1,0:T(8,128)(2,1)}, bf16[64,2048]{1,0:T(8,128)(2,1)S(1)}, u32[]{:S(2)}, u32[]{:S(2)}) collective-permute-start(bf16[64,2048]{1,0:T(8,128)(2,1)} %add_convert_fusion.1), channel_id=1, source_target_pairs={{8,0},{16,8},{24,16},{9,1},{17,9},{25,17},{10,2},{18,10},{26,18},{... | collective-permute-start | bytes 786440 | tf_op jit(solution)/shard_map/ppermute | solution.py:219
  73.1 9.7 %collective-permute-start.4 = (bf16[64,2048]{1,0:T(8,128)(2,1)S(1)}, bf16[64,2048]{1,0:T(8,128)(2,1)S(1)}, u32[]{:S(2)}, u32[]{:S(2)}) collective-permute-start(bf16[64,2048]{1,0:T(8,128)(2,1)S(1)} %add_convert_fusion), channel_id=1, source_target_pairs={{8,0},{16,8},{24,16},{9,1},{17,9},{25,17},{10,2},{18,10},{26,18},{... | collective-permute-start | bytes 786440 | tf_op jit(solution)/shard_map/ppermute | solution.py:219
  82.8 1.0 %copy-start.1 = (bf16[128,2048]{1,0:T(8,128)(2,1)S(1)}, bf16[128,2048]{1,0:T(8,128)(2,1)}, u32[]{:S(2)}) copy-start(bf16[128,2048]{1,0:T(8,128)(2,1)} %top_ref.1) | copy-start | bytes 1572868
  (3 other events, 2.0 us)
where the time goes:
time: 89 us; the launch traced here: 88.5 us
  waiting for transfers between devices  31.7 us (36%)
  Pallas kernels  30.9 us (35%)
  starting transfers between devices  18.1 us (20%)
  local copies, waits for them, and re-layouts  5.91 us (7%)
  other arithmetic  0.98 us (1%)
  between operations  0.92 us (1%)
    ppermute x4, waiting for transfers between devices, relay(): arrived.append(lax.ppermute(sent, axis, pairs))  17.9 us
    pallas_call x2, Pallas kernels, precondition(): pl.pallas_call(functools.partial(feature_kernel, pieces=pieces, place=pla...  15.2 us
    ppermute x13, waiting for transfers between devices, flipped(): return lax.ppermute(value, axis, [(k, k ^ bit) for k in range(count)])  13.8 us
    ppermute x13, starting transfers between devices, flipped(): return lax.ppermute(value, axis, [(k, k ^ bit) for k in range(count)])  12.8 us
    pallas_call x1, Pallas kernels, invert_value(): pl.pallas_call(functools.partial(value_kernel, pieces=len(pieces)), in_sp...  6.36 us
    unnamed x36, local copies, waits for them, and re-layouts  5.91 us
    ppermute x4, starting transfers between devices, relay(): arrived.append(lax.ppermute(sent, axis, pairs))  5.26 us
    pallas_call x1, Pallas kernels, upstream_of(): pl.pallas_call(functools.partial(upstream_kernel, position=position, capa...  4.24 us
  transfers between devices with their start and end apart: 17, of which 5 were waited for; matrix products, arithmetic and copies ran while one was open for 1% of the time, Pallas kernels for 31%

commit v1 on v0

--- a/solution.py
+++ b/solution.py
@@ -120,6 +120,7 @@
 SMEM = pl.BlockSpec(memory_space=pltpu.SMEM)
 VMEM = pl.BlockSpec(memory_space=pltpu.VMEM)
 HBM = pl.BlockSpec(memory_space=pltpu.HBM)
+ANY = pl.BlockSpec(memory_space=pl.ANY)
 
 
 def in_hbm(*arrays):
@@ -205,16 +206,35 @@
     return outs[0], outs[-1], outs[1 : 1 + blocks // 2], outs[1 + blocks // 2 : -1]
 
 
-def relay(term, first_sent, axis):
-    count, index = lax.axis_size(axis), lax.axis_index(axis)
-    rows = term.shape[0] // RELAY_CHUNKS
+def payload_kernel(section, term, arrived, out, *, wave, sections):
+    rows = out.shape[0]
+    chunk = wave - RELAY_LAG * (sections - 1 - section[0])
+    chunk = jnp.minimum(jnp.maximum(chunk, 0), RELAY_CHUNKS - 1)
+    own = term[pl.ds(pl.multiple_of(chunk * rows, rows), rows)].astype(jnp.float32)
+    out[...] = (own + arrived[...].astype(jnp.float32)).astype(jnp.bfloat16)
+
+
+def payload(section, term, arrived, wave, sections):
+    return pl.pallas_call(
+        functools.partial(payload_kernel, wave=wave, sections=sections),
+        in_specs=[SMEM, VMEM, VMEM],
+        out_specs=VMEM,
+        out_shape=jax.ShapeDtypeStruct(arrived.shape, jnp.bfloat16),
+        compiler_params=pltpu.CompilerParams(vmem_limit_bytes=VMEM_LIMIT),
+        cost_estimate=pl.CostEstimate(
+            flops=arrived.size, bytes_accessed=6 * arrived.size, transcendentals=0
+        ),
+        name="payload",
+    )(section, *in_vmem(term, arrived))
+
+
+def relay(term, first_sent, section, axis):
+    count = lax.axis_size(axis)
     arrived = []
     for wave in range(RELAY_CHUNKS + RELAY_LAG * (count - 2)):
-        chunk = jnp.clip(wave - RELAY_LAG * (count - 1 - index), 0, RELAY_CHUNKS - 1)
-        sent = lax.dynamic_slice_in_dim(term, chunk * rows, rows, 0) if wave else first_sent
+        sent = first_sent
         if wave >= RELAY_LAG:
-            before = arrived[wave - RELAY_LAG].astype(jnp.float32)
-            sent = (sent.astype(jnp.float32) + before).astype(jnp.bfloat16)
+            sent = payload(section, term, arrived[wave - RELAY_LAG], wave, count)
         pairs = [(k, k - 1) for k in range(1, count)]
         arrived.append(lax.ppermute(sent, axis, pairs))
     return arrived
@@ -261,60 +281,38 @@
     ]
 
 
-def row_copies(pieces, target, sems, first=0):
-    rows = target.shape[0] // len(pieces)
-    return [
-        pltpu.make_async_copy(piece, target.at[pl.ds(k * rows, rows)], sems.at[first + k])
-        for k, piece in enumerate(pieces)
-    ]
-
-
-def value_kernel(place, own_stats, other_stats, *refs, pieces):
-    span = pl.ds(pl.multiple_of(place[0] * BLOCK, BLOCK), BLOCK)
-    out, state, halves, tokens, sems = refs[pieces:]
-    copies = row_copies([ref.at[:, span] for ref in refs[:pieces]], tokens, sems)
-    for copy in copies:
-        copy.start()
-    for copy in copies:
-        copy.wait()
+def value_kernel(core, tensor, own_stats, other_stats, *refs, pieces):
+    span = pl.ds(pl.multiple_of(core[0] * BLOCK, BLOCK), BLOCK)
+    tokens = jnp.concatenate([ref[:, span] for ref in refs[:pieces]], axis=0)
+    out, state, halves = refs[pieces:]
     own_limit, other_limit = jnp.max(own_stats[2:3]), jnp.max(other_stats[2:3])
-    limit = jnp.where(place[0] == place[1], own_limit, other_limit).astype(jnp.int32)
-    out[...] = inverse_of(tokens[...], limit, state, halves)
-
-
-def invert_value(place, own_stats, other_stats, pieces):
+    limit = jnp.where(core[0] == tensor[0], own_limit, other_limit).astype(jnp.int32)
+    out[...] = inverse_of(tokens, limit, state, halves)
+
+
+def invert_value(core, tensor, own_stats, other_stats, pieces):
     return pl.pallas_call(
         functools.partial(value_kernel, pieces=len(pieces)),
-        in_specs=[SMEM, VMEM, VMEM] + [HBM] * len(pieces),
+        in_specs=[SMEM, SMEM] + [VMEM] * (2 + len(pieces)),
         out_specs=VMEM,
-        scratch_shapes=scratch()
-        + [
-            pltpu.VMEM((len(pieces) * pieces[0].shape[0], BLOCK), jnp.bfloat16),
-            pltpu.SemaphoreType.DMA((len(pieces),)),
-        ],
+        scratch_shapes=scratch(),
         out_shape=jax.ShapeDtypeStruct((BLOCK, BLOCK), jnp.bfloat16),
         compiler_params=pltpu.CompilerParams(vmem_limit_bytes=VMEM_LIMIT),
         cost_estimate=pl.CostEstimate(
             flops=22 * BLOCK**3, bytes_accessed=4 * BLOCK**2, transcendentals=0
         ),
         name="value_inverse",
-    )(place, *in_vmem(own_stats, other_stats), *in_hbm(*pieces))
+    )(core, tensor, *in_vmem(own_stats, other_stats, *pieces))
 
 
 def feature_kernel(core, table, counts, *refs, pieces, place, half_blocks, capacity):
+    normed = jnp.concatenate([ref[...] for ref in refs[:pieces]], axis=0)
     own_inverse, other_inverse = refs[2 * pieces], refs[2 * pieces + 1]
-    out, state, halves, left, normed, cotangent, sems = refs[-7:]
-    copies = row_copies(refs[:pieces], normed, sems)
-    later = row_copies(refs[pieces : 2 * pieces], cotangent, sems, pieces)
-    for copy in copies + later:
-        copy.start()
-    for copy in copies:
-        copy.wait()
+    out, state, halves, left = refs[-4:]
     owner = table[core[0] * half_blocks + place] // capacity
-    inverse = inverse_of(normed[...], counts[owner], state, halves)
-    for copy in later:
-        copy.wait()
-    grad = first_dim_product(normed[...], cotangent[...]).astype(jnp.bfloat16)
+    inverse = inverse_of(normed, counts[owner], state, halves)
+    cotangent = jnp.concatenate([ref[...] for ref in refs[pieces : 2 * pieces]], axis=0)
+    grad = first_dim_product(normed, cotangent).astype(jnp.bfloat16)
     left[...] = product(inverse, grad).astype(jnp.bfloat16)
     for turn, value_inverse in ((0, own_inverse), (1, other_inverse)):
         block = core[0] if turn == 0 else 1 - core[0]
@@ -325,27 +323,20 @@
 def precondition(core, table, counts, normed, cotangents, inverses, place, half_blocks, capacity):
     value_width = cotangents[0].shape[1]
     pieces = len(normed)
-    tokens = pieces * normed[0].shape[0]
     return pl.pallas_call(
         functools.partial(
             feature_kernel, pieces=pieces, place=place, half_blocks=half_blocks, capacity=capacity
         ),
-        in_specs=[SMEM] * 3 + [HBM] * (2 * pieces) + [VMEM] * 2,
+        in_specs=[SMEM] * 3 + [VMEM] * (2 * pieces + 2),
         out_specs=VMEM,
-        scratch_shapes=scratch()
-        + [
-            pltpu.VMEM((BLOCK, value_width), jnp.bfloat16),
-            pltpu.VMEM((tokens, BLOCK), jnp.bfloat16),
-            pltpu.VMEM((tokens, value_width), jnp.bfloat16),
-            pltpu.SemaphoreType.DMA((2 * pieces,)),
-        ],
+        scratch_shapes=scratch() + [pltpu.VMEM((BLOCK, value_width), jnp.bfloat16)],
         out_shape=jax.ShapeDtypeStruct((BLOCK, value_width), jnp.bfloat16),
         compiler_params=pltpu.CompilerParams(vmem_limit_bytes=VMEM_LIMIT),
         cost_estimate=pl.CostEstimate(
             flops=34 * BLOCK**3, bytes_accessed=8 * BLOCK**2, transcendentals=0
         ),
         name="precondition",
-    )(core, *in_hbm(table, counts, *normed, *cotangents), *in_vmem(*inverses))
+    )(core, *in_hbm(table, counts), *in_vmem(*normed, *cotangents, *inverses))
 
 
 def place_kernel(core, *refs, blocks):
@@ -406,7 +397,8 @@
     term, first_sent, mine, theirs = terms_of(
         core, scaled, acts, norm_gain, own_stats, other_stats, half_width * tensor_size
     )
-    arrived = relay(term, first_sent, "section")
+    section = lax.axis_index("section")[None]
+    arrived = relay(term, first_sent, section, "section")
 
     normed = []
     for own, sent in zip(mine, theirs):
@@ -415,8 +407,8 @@
             pieces.append(flipped(sent if mask % 2 else own, "dp", mask))
         normed.append(pieces)
 
-    place = jnp.stack([core[0], lax.axis_index("tensor")])
-    own_inverse = invert_value(place, own_stats, other_stats, cotangents)
+    tensor = lax.axis_index("tensor")[None]
+    own_inverse = invert_value(core, tensor, own_stats, other_stats, cotangents)
     inverses = [own_inverse, flipped(own_inverse, "dp", 1)]
 
     own_rows, received = [], []
@@ -428,7 +420,6 @@
         )
         received.append(flipped(own_rows[k], "dp", 1))
     output = place_rows(core, own_rows, received)
-    section = lax.axis_index("section")[None]
     input_grad = finish(section, lax.axis_size("section"), top_grad, term, arrived)
     return (input_grad[None], output[None])
 

time: 89 us -> 88.3 us (level)
  waiting for transfers between devices: 31.7 us -> 38.5 us
  Pallas kernels: 30.9 us -> 27.3 us
  local copies, waits for them, and re-layouts: 5.91 us -> 2.88 us
  other arithmetic: 0.98 us -> 0 us
    ppermute x4, waiting for transfers between devices: 17.9 us -> 25.4 us  [relay(): arrived.append(lax.ppermute(sent, axis, pairs))]
    unnamed x36 -> x22, local copies, waits for them, and re-layouts: 5.91 us -> 2.88 us
    pallas_call x2, Pallas kernels: 15.2 us -> 12.5 us  [precondition(): pl.pallas_call(functools.partial(feature_kernel, pieces=pieces, place=pla...]
    pallas_call x1, Pallas kernels: 6.36 us -> 4.7 us  [invert_value(): pl.pallas_call(functools.partial(value_kernel, pieces=len(pieces)), in_sp...]
    convert_element_type x3 -> x0, other arithmetic: 0.9 us -> none  [relay(): sent = (sent.astype(jnp.float32) + before).astype(jnp.bfloat16)]
  transfers between devices with their start and end apart: 17 -> 17, of which waited for: 5 -> 7; matrix products, arithmetic and copies ran while one was open for 1% -> 0% of each run, Pallas kernels for 31% -> 22%
where the time goes in v1:
time: 88.3 us; the launch traced here: 87.9 us
  waiting for transfers between devices  38.5 us (44%)
  Pallas kernels  27.3 us (31%)
  starting transfers between devices  18.4 us (21%)
  local copies, waits for them, and re-layouts  2.88 us (3%)
    ppermute x4, waiting for transfers between devices, relay(): arrived.append(lax.ppermute(sent, axis, pairs))  25.4 us
    ppermute x13, starting transfers between devices, flipped(): return lax.ppermute(value, axis, [(k, k ^ bit) for k in range(count)])  13.1 us
    ppermute x13, waiting for transfers between devices, flipped(): return lax.ppermute(value, axis, [(k, k ^ bit) for k in range(count)])  13.1 us
    pallas_call x2, Pallas kernels, precondition(): pl.pallas_call(functools.partial(feature_kernel, pieces=pieces, place=pla...  12.5 us
    ppermute x4, starting transfers between devices, relay(): arrived.append(lax.ppermute(sent, axis, pairs))  5.29 us
    pallas_call x1, Pallas kernels, invert_value(): pl.pallas_call(functools.partial(value_kernel, pieces=len(pieces)), in_sp...  4.7 us
    pallas_call x1, Pallas kernels, upstream_of(): pl.pallas_call(functools.partial(upstream_kernel, position=position, capa...  4.24 us
    pallas_call x1, Pallas kernels, place_rows(): pl.pallas_call(functools.partial(place_kernel, blocks=blocks), in_specs=[...  3.58 us
  transfers between devices with their start and end apart: 17, of which 7 were waited for; matrix products, arithmetic and copies ran while one was open for 0% of the time, Pallas kernels for 22%

profile of v1, /device:TPU:0, one launch (start us, length us, event | category | flops | bytes accessed | tf_op | source)
XLA Modules:
  0.0 87.9 jit_solution(5018154849285456188)
XLA Ops:
  0.6 3.0 %collective-permute-start.9 = (bf16[128,1024]{1,0:T(8,128)(2,1)}, bf16[128,1024]{1,0:T(8,128)(2,1)S(1)}, u32[]{:S(2)}, u32[]{:S(2)}) collective-permute-start(bf16[128,1024]{1,0:T(8,128)(2,1)} %bitcast.12), channel_id=1, source_target_pairs={{0,4},{2,6},{4,0},{6,2},{1,5},{3,7},{5,1},{7,3},{8,12},{10,14},{12... | collective-permute-start | bytes 786440 | tf_op jit(solution)/shard_map/ppermute | solution.py:23
  3.7 6.5 %collective-permute-done.9.refs_2_.refs_6_ = bf16[128,1024]{1,0:T(8,128)(2,1)S(1)} collective-permute-done((bf16[128,1024]{1,0:T(8,128)(2,1)}, bf16[128,1024]{1,0:T(8,128)(2,1)S(1)}, u32[]{:S(2)}, u32[]{:S(2)}) %collective-permute-start.9) | collective-permute-done | bytes 262176 | tf_op jit(solution)/shard_map/ppermute | solution.py:23
  10.2 4.2 %upstream.1 = (f32[128,2048]{1,0:T(8,128)S(1)}, f32[8,128]{1,0:T(8,128)S(1)}) custom-call(s32[13]{0:T(128)} %bitcast.21, s32[4]{0:T(128)} %bitcast.24, bf16[128,1024]{1,0:T(8,128)(2,1)} %bitcast.14, bf16[2048,1024]{1,0:T(8,128)(2,1)} %bitcast.18, bf16[128,2048]{1,0:T(8,128)(2,1)} %bitcast.10, f32[1,2048]{1,0:T(1,128)} %gain_ref.1), custom_call_target="tpu_custom_call" | custom-call | flops 536870912 | bytes 6291456 | tf_op jit(solution)/shard_map/upstream/pallas_call | solution.py:137
  14.4 1.8 %collective-permute-start = (f32[8,128]{1,0:T(8,128)S(1)}, f32[8,128]{1,0:T(8,128)S(1)}, u32[]{:S(2)}, u32[]{:S(2)}) collective-permute-start(f32[8,128]{1,0:T(8,128)S(1)} %get-tuple-element.11.own_ref.own_stats), channel_id=1, source_target_pairs={{0,1},{1,0},{2,3},{3,2},{4,5},{5,4},{6,7},{7,6},{8,9},{9,8},{10,11... | collective-permute-start | bytes 12296 | tf_op jit(solution)/shard_map/ppermute | solution.py:23
  16.3 1.8 %collective-permute-done.other_ref.other_stats = f32[8,128]{1,0:T(8,128)S(1)} collective-permute-done((f32[8,128]{1,0:T(8,128)S(1)}, f32[8,128]{1,0:T(8,128)S(1)}, u32[]{:S(2)}, u32[]{:S(2)}) %collective-permute-start) | collective-permute-done | bytes 4128 | tf_op jit(solution)/shard_map/ppermute | solution.py:23
  18.2 4.7 %value_inverse.1.refs_8_ = bf16[512,512]{1,0:T(8,128)(2,1)S(1)} custom-call(s32[1]{0:T(128)} %bitcast.1.core, s32[1]{0:T(128)} %bitcast.8.tensor, f32[8,128]{1,0:T(8,128)S(1)} %get-tuple-element.11.own_ref.own_stats, f32[8,128]{1,0:T(8,128)S(1)} %collective-permute-done.other_ref.other_stats, bf16[128,1024]{1,0:T(8,128)(2,1)S(1)} %bitcast.15, ...), custom_call_target="tpu_custom_call" | custom-call | flops 2952790016 | bytes 1048576 | tf_op jit(solution)/shard_map/value_inverse/pallas_call | solution.py:294
  22.9 0.1 collective-permute-start.11
  23.0 1.0 %terms.1 = (bf16[128,2048]{1,0:T(8,128)(2,1)S(1)}, bf16[128,512]{1,0:T(8,128)(2,1)S(1)}, bf16[128,512]{1,0:T(8,128)(2,1)S(1)}, bf16[128,512]{1,0:T(8,128)(2,1)S(...) custom-call(s32[1]{0:T(128)} %bitcast.1.core, f32[128,2048]{1,0:T(8,128)S(1)} %get-tuple-element.10.scaled_ref, ...), custom_call_target="tpu_custom_call" | custom-call | flops 2097152 | bytes 2621440 | tf_op jit(solution)/shard_map/terms/pallas_call | solution.py:192
  24.0 1.7 %collective-permute-start.6 = (bf16[128,512]{1,0:T(8,128)(2,1)S(1)}, bf16[128,512]{1,0:T(8,128)(2,1)S(1)}, u32[]{:S(2)}, u32[]{:S(2)}) collective-permute-start(bf16[128,512]{1,0:T(8,128)(2,1)S(1)} %get-tuple-element.14.refs_0_), channel_id=1, source_target_pairs={{0,4},{2,6},{4,0},{6,2},{1,5},{3,7},{5,1},{7,3},{8,12},{10,14},{12... | collective-permute-start | bytes 393224 | tf_op jit(solution)/shard_map/ppermute | solution.py:23
  25.7 0.1 collective-permute-start.7
  25.8 0.3 collective-permute-start.5
  26.1 1.5 %collective-permute-start.14 = (bf16[128,512]{1,0:T(8,128)(2,1)S(1)}, bf16[128,512]{1,0:T(8,128)(2,1)S(1)}, u32[]{:S(2)}, u32[]{:S(2)}) collective-permute-start(bf16[128,512]{1,0:T(8,128)(2,1)S(1)} %get-tuple-element.17), channel_id=1, source_target_pairs={{0,6},{2,4},{4,2},{6,0},{1,7},{3,5},{5,3},{7,1},{8,14},{10,12},{12... | collective-permute-start | bytes 393224 | tf_op jit(solution)/shard_map/ppermute | solution.py:23
  27.7 2.7 %collective-permute-done.6.refs_2_ = bf16[128,512]{1,0:T(8,128)(2,1)S(1)} collective-permute-done((bf16[128,512]{1,0:T(8,128)(2,1)S(1)}, bf16[128,512]{1,0:T(8,128)(2,1)S(1)}, u32[]{:S(2)}, u32[]{:S(2)}) %collective-permute-start.6) | collective-permute-done | bytes 131104 | tf_op jit(solution)/shard_map/ppermute | solution.py:23
  30.4 2.1 %collective-permute-done.7.refs_3_ = bf16[128,512]{1,0:T(8,128)(2,1)S(1)} collective-permute-done((bf16[128,512]{1,0:T(8,128)(2,1)S(1)}, bf16[128,512]{1,0:T(8,128)(2,1)S(1)}, u32[]{:S(2)}, u32[]{:S(2)}) %collective-permute-start.7) | collective-permute-done | bytes 131104 | tf_op jit(solution)/shard_map/ppermute | solution.py:23
  32.4 1.5 %collective-permute-start.13 = (bf16[128,512]{1,0:T(8,128)(2,1)S(1)}, bf16[128,512]{1,0:T(8,128)(2,1)S(1)}, u32[]{:S(2)}, u32[]{:S(2)}) collective-permute-start(bf16[128,512]{1,0:T(8,128)(2,1)S(1)} %get-tuple-element.16.refs_0_), channel_id=1, source_target_pairs={{0,4},{2,6},{4,0},{6,2},{1,5},{3,7},{5,1},{7,3},{8,12},{10,14},{12... | collective-permute-start | bytes 393224 | tf_op jit(solution)/shard_map/ppermute | solution.py:23
  33.9 1.4 %collective-permute-start.1 = (bf16[64,2048]{1,0:T(8,128)(2,1)}, bf16[64,2048]{1,0:T(8,128)(2,1)S(1)}, u32[]{:S(2)}, u32[]{:S(2)}) collective-permute-start(bf16[64,2048]{1,0:T(8,128)(2,1)} %get-tuple-element.13), channel_id=1, source_target_pairs={{8,0},{16,8},{24,16},{9,1},{17,9},{25,17},{10,2},{18,10},{26,18},{... | collective-permute-start | bytes 786440 | tf_op jit(solution)/shard_map/ppermute | solution.py:239
  35.4 5.0 %precondition.2.refs_0_ = bf16[512,1024]{1,0:T(8,128)(2,1)S(1)} custom-call(s32[1]{0:T(128)} %bitcast.1.core, s32[13]{0:T(128)} %bitcast.22, s32[4]{0:T(128)} %bitcast.25, bf16[128,512]{1,0:T(8,128)(2,1)S(1)} %get-tuple-element.14.refs_0_, bf16[128,512]{1,0:T(8,128)(2,1)S(1)} %collective-permute-done.5.refs_1_, ...), custom_call_target="tpu_custom_call" | custom-call | flops 4563402752 | bytes 2097152 | tf_op jit(solution)/shard_map/precondition/pallas_call | solution.py:326
  40.4 3.0 %collective-permute-start.15 = (bf16[512,1024]{1,0:T(8,128)(2,1)S(1)}, bf16[512,1024]{1,0:T(8,128)(2,1)S(1)}, u32[]{:S(2)}, u32[]{:S(2)}) collective-permute-start(bf16[512,1024]{1,0:T(8,128)(2,1)S(1)} %precondition.2.refs_0_), channel_id=1, source_target_pairs={{0,2},{2,0},{4,6},{6,4},{1,3},{3,1},{5,7},{7,5},{8,10},{10,8},{12,... | collective-permute-start | bytes 3145736 | tf_op jit(solution)/shard_map/ppermute | solution.py:23
  43.5 0.9 %copy-done.6 = bf16[128,1024]{1,0:T(8,128)(2,1)S(1)} copy-done((bf16[128,1024]{1,0:T(8,128)(2,1)S(1)}, bf16[128,1024]{1,0:T(8,128)(2,1)}, u32[]{:S(2)}) %copy-start.6) | copy-done | bytes 262168
  44.4 0.9 %copy-done.8 = bf16[128,1024]{1,0:T(8,128)(2,1)S(1)} copy-done((bf16[128,1024]{1,0:T(8,128)(2,1)S(1)}, bf16[128,1024]{1,0:T(8,128)(2,1)}, u32[]{:S(2)}) %copy-start.8) | copy-done | bytes 262168
  45.4 0.9 %copy-done.10 = bf16[128,1024]{1,0:T(8,128)(2,1)S(1)} copy-done((bf16[128,1024]{1,0:T(8,128)(2,1)S(1)}, bf16[128,1024]{1,0:T(8,128)(2,1)}, u32[]{:S(2)}) %copy-start.10) | copy-done | bytes 262168
  46.3 7.4 %precondition.3.refs_1_ = bf16[512,1024]{1,0:T(8,128)(2,1)} custom-call(s32[1]{0:T(128)} %bitcast.1.core, s32[13]{0:T(128)} %bitcast.23, s32[4]{0:T(128)} %bitcast.26, bf16[128,512]{1,0:T(8,128)(2,1)S(1)} %get-tuple-element.16.refs_0_, bf16[128,512]{1,0:T(8,128)(2,1)S(1)} %collective-permute-done.12.refs_1_, ...), custom_call_target="tpu_custom_call" | custom-call | flops 4563402752 | bytes 2097152 | tf_op jit(solution)/shard_map/precondition/pallas_call | solution.py:326
  53.7 0.1 payload.3
  53.8 1.3 %collective-permute-start.2 = (bf16[64,2048]{1,0:T(8,128)(2,1)S(1)}, bf16[64,2048]{1,0:T(8,128)(2,1)S(1)}, u32[]{:S(2)}, u32[]{:S(2)}) collective-permute-start(bf16[64,2048]{1,0:T(8,128)(2,1)S(1)} %payload.3), channel_id=1, source_target_pairs={{8,0},{16,8},{24,16},{9,1},{17,9},{25,17},{10,2},{18,10},{26,18},{... | collective-permute-start | bytes 786440 | tf_op jit(solution)/shard_map/ppermute | solution.py:239
  55.1 9.3 %collective-permute-done.2.arrived.refs_1_ = bf16[64,2048]{1,0:T(8,128)(2,1)S(1)} collective-permute-done((bf16[64,2048]{1,0:T(8,128)(2,1)S(1)}, bf16[64,2048]{1,0:T(8,128)(2,1)S(1)}, u32[]{:S(2)}, u32[]{:S(2)}) %collective-permute-start.2) | collective-permute-done | bytes 262176 | tf_op jit(solution)/shard_map/ppermute | solution.py:239
  64.4 0.1 payload.4
  64.5 1.3 %collective-permute-start.3 = (bf16[64,2048]{1,0:T(8,128)(2,1)S(1)}, bf16[64,2048]{1,0:T(8,128)(2,1)S(1)}, u32[]{:S(2)}, u32[]{:S(2)}) collective-permute-start(bf16[64,2048]{1,0:T(8,128)(2,1)S(1)} %payload.4), channel_id=1, source_target_pairs={{8,0},{16,8},{24,16},{9,1},{17,9},{25,17},{10,2},{18,10},{26,18},{... | collective-permute-start | bytes 786440 | tf_op jit(solution)/shard_map/ppermute | solution.py:239
  65.8 8.5 %collective-permute-done.3.arrived.refs_2_ = bf16[64,2048]{1,0:T(8,128)(2,1)S(1)} collective-permute-done((bf16[64,2048]{1,0:T(8,128)(2,1)S(1)}, bf16[64,2048]{1,0:T(8,128)(2,1)S(1)}, u32[]{:S(2)}, u32[]{:S(2)}) %collective-permute-start.3) | collective-permute-done | bytes 262176 | tf_op jit(solution)/shard_map/ppermute | solution.py:239
  74.3 1.3 %collective-permute-start.4 = (bf16[64,2048]{1,0:T(8,128)(2,1)S(1)}, bf16[64,2048]{1,0:T(8,128)(2,1)S(1)}, u32[]{:S(2)}, u32[]{:S(2)}) collective-permute-start(bf16[64,2048]{1,0:T(8,128)(2,1)S(1)} %payload.5), channel_id=1, source_target_pairs={{8,0},{16,8},{24,16},{9,1},{17,9},{25,17},{10,2},{18,10},{26,18},{... | collective-permute-start | bytes 786440 | tf_op jit(solution)/shard_map/ppermute | solution.py:239
  75.6 7.6 %collective-permute-done.4.refs_3_ = bf16[64,2048]{1,0:T(8,128)(2,1)S(1)} collective-permute-done((bf16[64,2048]{1,0:T(8,128)(2,1)S(1)}, bf16[64,2048]{1,0:T(8,128)(2,1)S(1)}, u32[]{:S(2)}, u32[]{:S(2)}) %collective-permute-start.4) | collective-permute-done | bytes 262176 | tf_op jit(solution)/shard_map/ppermute | solution.py:239
  83.2 1.1 %finish.1 = bf16[128,2048]{1,0:T(8,128)(2,1)} custom-call(s32[1]{0:T(128)} %bitcast.section, bf16[128,2048]{1,0:T(8,128)(2,1)S(1)} %copy-done.1, bf16[128,2048]{1,0:T(8,128)(2,1)S(1)} %get-tuple-element.12.term.term_ref, bf16[64,2048]{1,0:T(8,128)(2,1)S(1)} %collective-permute-done.1.arrived.refs_0_, ...), custom_call_target="tpu_custom_call" | custom-call | flops 524288 | bytes 2097152 | tf_op jit(solution)/shard_map/finish/pallas_call | solution.py:264
  84.3 3.6 %place_rows.1 = bf16[2048,1024]{1,0:T(8,128)(2,1)} custom-call(s32[1]{0:T(128)} %bitcast.1.core, bf16[512,1024]{1,0:T(8,128)(2,1)S(1)} %precondition.2.refs_0_, bf16[512,1024]{1,0:T(8,128)(2,1)} %precondition.3.refs_1_, bf16[512,1024]{1,0:T(8,128)(2,1)S(1)} %collective-permute-done.15.refs_2_, bf16[512,1024]{1,0:T(8,128)(2,1)} %collective-permute-done.16.refs_3_), custom_call_target="tpu_custom_call" | custom-call | bytes 8388608 | tf_op jit(solution)/shard_map/place_rows/pallas_call | solution.py:358
  (34 shorter events, 0.1 us)
Async XLA Ops:
  0.6 17.5 %copy-start.2 = (bf16[1,128,1024]{2,1,0:T(8,128)(2,1)S(1)}, bf16[1,128,1024]{2,1,0:T(8,128)(2,1)}, u32[]{:S(2)}) copy-start(bf16[1,128,1024]{2,1,0:T(8,128)(2,1)} %param.10) | copy-start | bytes 786436
  0.6 9.6 %collective-permute-start.9 = (bf16[128,1024]{1,0:T(8,128)(2,1)}, bf16[128,1024]{1,0:T(8,128)(2,1)S(1)}, u32[]{:S(2)}, u32[]{:S(2)}) collective-permute-start(bf16[128,1024]{1,0:T(8,128)(2,1)} %bitcast.12), channel_id=1, source_target_pairs={{0,4},{2,6},{4,0},{6,2},{1,5},{3,7},{5,1},{7,3},{8,12},{10,14},{12... | collective-permute-start | bytes 786440 | tf_op jit(solution)/shard_map/ppermute | solution.py:23
  3.7 14.4 %collective-permute-start.8 = (bf16[128,1024]{1,0:T(8,128)(2,1)}, bf16[128,1024]{1,0:T(8,128)(2,1)S(1)}, u32[]{:S(2)}, u32[]{:S(2)}) collective-permute-start(bf16[128,1024]{1,0:T(8,128)(2,1)} %bitcast.13), channel_id=1, source_target_pairs={{0,2},{2,0},{4,6},{6,4},{1,3},{3,1},{5,7},{7,5},{8,10},{10,8},{12,... | collective-permute-start | bytes 786440 | tf_op jit(solution)/shard_map/ppermute | solution.py:23
  10.2 25.2 %copy-start.5 = (bf16[128,1024]{1,0:T(8,128)(2,1)}, bf16[128,1024]{1,0:T(8,128)(2,1)S(1)}, u32[]{:S(2)}) copy-start(bf16[128,1024]{1,0:T(8,128)(2,1)S(1)} %collective-permute-done.9.refs_2_.refs_6_) | copy-start | bytes 786436
  10.2 7.9 %collective-permute-start.10 = (bf16[128,1024]{1,0:T(8,128)(2,1)S(1)}, bf16[128,1024]{1,0:T(8,128)(2,1)S(1)}, u32[]{:S(2)}, u32[]{:S(2)}) collective-permute-start(bf16[128,1024]{1,0:T(8,128)(2,1)S(1)} %collective-permute-done.9.refs_2_.refs_6_), channel_id=1, source_target_pairs={{0,2},{2,0},{4,6},{6,4},{1,3},{3,1},{5,7},{7,5},{8,10},{10,8},{12,... | collective-permute-start | bytes 786440 | tf_op jit(solution)/shard_map/ppermute | solution.py:23
  14.4 3.7 %collective-permute-start = (f32[8,128]{1,0:T(8,128)S(1)}, f32[8,128]{1,0:T(8,128)S(1)}, u32[]{:S(2)}, u32[]{:S(2)}) collective-permute-start(f32[8,128]{1,0:T(8,128)S(1)} %get-tuple-element.11.own_ref.own_stats), channel_id=1, source_target_pairs={{0,1},{1,0},{2,3},{3,2},{4,5},{5,4},{6,7},{7,6},{8,9},{9,8},{10,11... | collective-permute-start | bytes 12296 | tf_op jit(solution)/shard_map/ppermute | solution.py:23
  18.1 17.2 %copy-start.7 = (bf16[128,1024]{1,0:T(8,128)(2,1)}, bf16[128,1024]{1,0:T(8,128)(2,1)S(1)}, u32[]{:S(2)}) copy-start(bf16[128,1024]{1,0:T(8,128)(2,1)S(1)} %collective-permute-done.8.refs_1_.refs_5_) | copy-start | bytes 786436
  18.1 17.2 %copy-start.9 = (bf16[128,1024]{1,0:T(8,128)(2,1)}, bf16[128,1024]{1,0:T(8,128)(2,1)S(1)}, u32[]{:S(2)}) copy-start(bf16[128,1024]{1,0:T(8,128)(2,1)S(1)} %collective-permute-done.10.refs_3_.refs_7_) | copy-start | bytes 786436
  18.2 4.8 %copy-start = (bf16[1,128,2048]{2,1,0:T(8,128)(2,1)S(1)}, bf16[1,128,2048]{2,1,0:T(8,128)(2,1)}, u32[]{:S(2)}) copy-start(bf16[1,128,2048]{2,1,0:T(8,128)(2,1)} %param.7) | copy-start | bytes 1572868
  18.2 4.8 %copy-start.4 = (f32[1,2048]{1,0:T(1,128)S(1)}, f32[1,2048]{1,0:T(1,128)}, u32[]{:S(2)}) copy-start(f32[1,2048]{1,0:T(1,128)} %gain_ref.1) | copy-start | bytes 24580
  22.9 12.5 %collective-permute-start.11 = (bf16[512,512]{1,0:T(8,128)(2,1)S(1)}, bf16[512,512]{1,0:T(8,128)(2,1)S(1)}, u32[]{:S(2)}, u32[]{:S(2)}) collective-permute-start(bf16[512,512]{1,0:T(8,128)(2,1)S(1)} %value_inverse.1.refs_8_), channel_id=1, source_target_pairs={{0,2},{2,0},{4,6},{6,4},{1,3},{3,1},{5,7},{7,5},{8,10},{10,8},{12,... | collective-permute-start | bytes 1572872 | tf_op jit(solution)/shard_map/ppermute | solution.py:23
  24.0 6.4 %collective-permute-start.6 = (bf16[128,512]{1,0:T(8,128)(2,1)S(1)}, bf16[128,512]{1,0:T(8,128)(2,1)S(1)}, u32[]{:S(2)}, u32[]{:S(2)}) collective-permute-start(bf16[128,512]{1,0:T(8,128)(2,1)S(1)} %get-tuple-element.14.refs_0_), channel_id=1, source_target_pairs={{0,4},{2,6},{4,0},{6,2},{1,5},{3,7},{5,1},{7,3},{8,12},{10,14},{12... | collective-permute-start | bytes 393224 | tf_op jit(solution)/shard_map/ppermute | solution.py:23
  25.7 6.7 %collective-permute-start.7 = (bf16[128,512]{1,0:T(8,128)(2,1)S(1)}, bf16[128,512]{1,0:T(8,128)(2,1)S(1)}, u32[]{:S(2)}, u32[]{:S(2)}) collective-permute-start(bf16[128,512]{1,0:T(8,128)(2,1)S(1)} %get-tuple-element.15), channel_id=1, source_target_pairs={{0,6},{2,4},{4,2},{6,0},{1,7},{3,5},{5,3},{7,1},{8,14},{10,12},{12... | collective-permute-start | bytes 393224 | tf_op jit(solution)/shard_map/ppermute | solution.py:23
  25.8 8.1 %collective-permute-start.5 = (bf16[128,512]{1,0:T(8,128)(2,1)S(1)}, bf16[128,512]{1,0:T(8,128)(2,1)S(1)}, u32[]{:S(2)}, u32[]{:S(2)}) collective-permute-start(bf16[128,512]{1,0:T(8,128)(2,1)S(1)} %get-tuple-element.15), channel_id=1, source_target_pairs={{0,2},{2,0},{4,6},{6,4},{1,3},{3,1},{5,7},{7,5},{8,10},{10,8},{12,... | collective-permute-start | bytes 393224 | tf_op jit(solution)/shard_map/ppermute | solution.py:23
  26.1 17.3 %collective-permute-start.14 = (bf16[128,512]{1,0:T(8,128)(2,1)S(1)}, bf16[128,512]{1,0:T(8,128)(2,1)S(1)}, u32[]{:S(2)}, u32[]{:S(2)}) collective-permute-start(bf16[128,512]{1,0:T(8,128)(2,1)S(1)} %get-tuple-element.17), channel_id=1, source_target_pairs={{0,6},{2,4},{4,2},{6,0},{1,7},{3,5},{5,3},{7,1},{8,14},{10,12},{12... | collective-permute-start | bytes 393224 | tf_op jit(solution)/shard_map/ppermute | solution.py:23
  30.3 13.1 %collective-permute-start.12 = (bf16[128,512]{1,0:T(8,128)(2,1)S(1)}, bf16[128,512]{1,0:T(8,128)(2,1)S(1)}, u32[]{:S(2)}, u32[]{:S(2)}) collective-permute-start(bf16[128,512]{1,0:T(8,128)(2,1)S(1)} %get-tuple-element.17), channel_id=1, source_target_pairs={{0,2},{2,0},{4,6},{6,4},{1,3},{3,1},{5,7},{7,5},{8,10},{10,8},{12,... | collective-permute-start | bytes 393224 | tf_op jit(solution)/shard_map/ppermute | solution.py:23
  32.4 11.0 %collective-permute-start.13 = (bf16[128,512]{1,0:T(8,128)(2,1)S(1)}, bf16[128,512]{1,0:T(8,128)(2,1)S(1)}, u32[]{:S(2)}, u32[]{:S(2)}) collective-permute-start(bf16[128,512]{1,0:T(8,128)(2,1)S(1)} %get-tuple-element.16.refs_0_), channel_id=1, source_target_pairs={{0,4},{2,6},{4,0},{6,2},{1,5},{3,7},{5,1},{7,3},{8,12},{10,14},{12... | collective-permute-start | bytes 393224 | tf_op jit(solution)/shard_map/ppermute | solution.py:23
  33.9 9.5 %copy-start.3 = (bf16[1,128,1024]{2,1,0:T(8,128)(2,1)S(1)}, bf16[1,128,1024]{2,1,0:T(8,128)(2,1)}, u32[]{:S(2)}) copy-start(bf16[1,128,1024]{2,1,0:T(8,128)(2,1)} %param.10) | copy-start | bytes 786436
  33.9 19.8 %collective-permute-start.1 = (bf16[64,2048]{1,0:T(8,128)(2,1)}, bf16[64,2048]{1,0:T(8,128)(2,1)S(1)}, u32[]{:S(2)}, u32[]{:S(2)}) collective-permute-start(bf16[64,2048]{1,0:T(8,128)(2,1)} %get-tuple-element.13), channel_id=1, source_target_pairs={{8,0},{16,8},{24,16},{9,1},{17,9},{25,17},{10,2},{18,10},{26,18},{... | collective-permute-start | bytes 786440 | tf_op jit(solution)/shard_map/ppermute | solution.py:239
  40.4 42.8 %copy-start.1 = (bf16[128,2048]{1,0:T(8,128)(2,1)S(1)}, bf16[128,2048]{1,0:T(8,128)(2,1)}, u32[]{:S(2)}) copy-start(bf16[128,2048]{1,0:T(8,128)(2,1)} %top_ref.1) | copy-start | bytes 1572868
  40.4 43.9 %collective-permute-start.15 = (bf16[512,1024]{1,0:T(8,128)(2,1)S(1)}, bf16[512,1024]{1,0:T(8,128)(2,1)S(1)}, u32[]{:S(2)}, u32[]{:S(2)}) collective-permute-start(bf16[512,1024]{1,0:T(8,128)(2,1)S(1)} %precondition.2.refs_0_), channel_id=1, source_target_pairs={{0,2},{2,0},{4,6},{6,4},{1,3},{3,1},{5,7},{7,5},{8,10},{10,8},{12,... | collective-permute-start | bytes 3145736 | tf_op jit(solution)/shard_map/ppermute | solution.py:23
  43.5 1.0 %copy-start.6 = (bf16[128,1024]{1,0:T(8,128)(2,1)S(1)}, bf16[128,1024]{1,0:T(8,128)(2,1)}, u32[]{:S(2)}) copy-start(bf16[128,1024]{1,0:T(8,128)(2,1)} %copy-done.5) | copy-start | bytes 786436
  44.4 0.9 %copy-start.8 = (bf16[128,1024]{1,0:T(8,128)(2,1)S(1)}, bf16[128,1024]{1,0:T(8,128)(2,1)}, u32[]{:S(2)}) copy-start(bf16[128,1024]{1,0:T(8,128)(2,1)} %copy-done.7) | copy-start | bytes 786436
  45.4 0.9 %copy-start.10 = (bf16[128,1024]{1,0:T(8,128)(2,1)S(1)}, bf16[128,1024]{1,0:T(8,128)(2,1)}, u32[]{:S(2)}) copy-start(bf16[128,1024]{1,0:T(8,128)(2,1)} %copy-done.9) | copy-start | bytes 786436
  53.7 30.6 %collective-permute-start.16 = (bf16[512,1024]{1,0:T(8,128)(2,1)}, bf16[512,1024]{1,0:T(8,128)(2,1)}, u32[]{:S(2)}, u32[]{:S(2)}) collective-permute-start(bf16[512,1024]{1,0:T(8,128)(2,1)} %precondition.3.refs_1_), channel_id=1, source_target_pairs={{0,2},{2,0},{4,6},{6,4},{1,3},{3,1},{5,7},{7,5},{8,10},{10,8},{12,... | collective-permute-start | bytes 3145736 | tf_op jit(solution)/shard_map/ppermute | solution.py:23
  53.8 10.6 %collective-permute-start.2 = (bf16[64,2048]{1,0:T(8,128)(2,1)S(1)}, bf16[64,2048]{1,0:T(8,128)(2,1)S(1)}, u32[]{:S(2)}, u32[]{:S(2)}) collective-permute-start(bf16[64,2048]{1,0:T(8,128)(2,1)S(1)} %payload.3), channel_id=1, source_target_pairs={{8,0},{16,8},{24,16},{9,1},{17,9},{25,17},{10,2},{18,10},{26,18},{... | collective-permute-start | bytes 786440 | tf_op jit(solution)/shard_map/ppermute | solution.py:239
  64.5 9.8 %collective-permute-start.3 = (bf16[64,2048]{1,0:T(8,128)(2,1)S(1)}, bf16[64,2048]{1,0:T(8,128)(2,1)S(1)}, u32[]{:S(2)}, u32[]{:S(2)}) collective-permute-start(bf16[64,2048]{1,0:T(8,128)(2,1)S(1)} %payload.4), channel_id=1, source_target_pairs={{8,0},{16,8},{24,16},{9,1},{17,9},{25,17},{10,2},{18,10},{26,18},{... | collective-permute-start | bytes 786440 | tf_op jit(solution)/shard_map/ppermute | solution.py:239
  74.3 8.9 %collective-permute-start.4 = (bf16[64,2048]{1,0:T(8,128)(2,1)S(1)}, bf16[64,2048]{1,0:T(8,128)(2,1)S(1)}, u32[]{:S(2)}, u32[]{:S(2)}) collective-permute-start(bf16[64,2048]{1,0:T(8,128)(2,1)S(1)} %payload.5), channel_id=1, source_target_pairs={{8,0},{16,8},{24,16},{9,1},{17,9},{25,17},{10,2},{18,10},{26,18},{... | collective-permute-start | bytes 786440 | tf_op jit(solution)/shard_map/ppermute | solution.py:239

commit v2 on v1

--- a/solution.py
+++ b/solution.py
@@ -47,14 +47,16 @@
     diagonal = rows == columns
     matrix = first_dim_product(tokens, tokens) * (1.0 / count)
     matrix = matrix + jnp.where(diagonal, DAMPING, 0.0)
+    state[0] = matrix
+    halves[0:order] = matrix.astype(jnp.bfloat16)
+    square = product(halves[0:order], halves[0:order])
     scale = lax.rsqrt(jnp.sum(matrix * matrix))
-    first = matrix * scale
+    first = state[0] * scale
+    grown = 2.0 * first - (scale * scale) * square
     start = jnp.where(diagonal, 2.0, 0.0) - first
-    first_half = first.astype(jnp.bfloat16)
     state[0] = start
+    state[1] = grown
     halves[0:order] = start.astype(jnp.bfloat16)
-    grown = 2.0 * first - product(first_half, first_half)
-    state[1] = grown
     halves[order:] = grown.astype(jnp.bfloat16)
 
     def sweep(k, carry):
@@ -73,18 +75,19 @@
 
 
 def upstream_kernel(
-    table, counts, cot_hbm, weight_hbm, act_hbm, gain_hbm, scaled_ref, stats_ref, cot, weight, act, gain, sems, *, position, capacity
+    table, counts, cot_hbm, weight_hbm, act_hbm, gain_hbm, scaled_ref, stats_ref, act, gain, cot, weight, sems, *, position, capacity
 ):
     tokens, width = act.shape
-    blocks = width // BLOCK
+    size = BLOCK
+    blocks = width // size
     small = [
         pltpu.make_async_copy(source, target, sems.at[k])
         for k, (source, target) in enumerate(((act_hbm, act), (cot_hbm, cot), (gain_hbm, gain)))
     ]
     large = [
         pltpu.make_async_copy(
-            weight_hbm.at[pl.ds(k * BLOCK, BLOCK)],
-            weight.at[pl.ds(k * BLOCK, BLOCK)],
+            weight_hbm.at[pl.ds(k * size, size)],
+            weight.at[pl.ds(k * size, size)],
             sems.at[3 + k],
         )
         for k in range(blocks)
@@ -103,16 +106,16 @@
     small[2].wait()
     inner = jnp.zeros((tokens, LANES), jnp.float32)
     for k in range(blocks):
-        span = slice(k * BLOCK, (k + 1) * BLOCK)
+        span = slice(k * size, (k + 1) * size)
         large[k].wait()
         upstream = lax.dot_general(
             cot[...], weight[span], (((1,), (1,)), ((), ())), preferred_element_type=jnp.float32
         )
         scaled = upstream * gain[:, span]
         scaled_ref[:, span] = scaled
-        for j in range(BLOCK // LANES):
+        for j in range(size // LANES):
             lanes = slice(j * LANES, (j + 1) * LANES)
-            start = k * BLOCK + j * LANES
+            start = k * size + j * LANES
             inner += scaled[:, lanes] * act[:, start : start + LANES].astype(jnp.float32)
     stats_ref[1:2] = jnp.sum(inner.T, axis=0, keepdims=True)
 
@@ -137,16 +140,16 @@
     return pl.pallas_call(
         functools.partial(upstream_kernel, position=position, capacity=capacity),
         in_specs=[SMEM, SMEM, HBM, HBM, HBM, HBM],
-        out_specs=[VMEM, VMEM],
+        out_specs=[VMEM] * 4,
         out_shape=[
             jax.ShapeDtypeStruct((tokens, width), jnp.float32),
             jax.ShapeDtypeStruct((STAT_ROWS, tokens), jnp.float32),
+            jax.ShapeDtypeStruct(activations.shape, activations.dtype),
+            jax.ShapeDtypeStruct(gain.shape, gain.dtype),
         ],
         scratch_shapes=[
             pltpu.VMEM(cotangent.shape, cotangent.dtype),
             pltpu.VMEM(weights.shape, weights.dtype),
-            pltpu.VMEM(activations.shape, activations.dtype),
-            pltpu.VMEM(gain.shape, gain.dtype),
             pltpu.SemaphoreType.DMA((3 + width // BLOCK,)),
         ],
         compiler_params=pltpu.CompilerParams(vmem_limit_bytes=VMEM_LIMIT),
@@ -235,7 +238,11 @@
         sent = first_sent
         if wave >= RELAY_LAG:
             sent = payload(section, term, arrived[wave - RELAY_LAG], wave, count)
-        pairs = [(k, k - 1) for k in range(1, count)]
+        pairs = [
+            (k, k - 1)
+            for k in range(1, count)
+            if 0 <= wave - RELAY_LAG * (count - 1 - k) < RELAY_CHUNKS
+        ]
         arrived.append(lax.ppermute(sent, axis, pairs))
     return arrived
 
@@ -390,12 +397,12 @@
     for piece in far:
         cotangents += [piece, flipped(piece, "dp", 1)]
 
-    scaled, own_stats = upstream_of(
+    scaled, own_stats, local_acts, local_gain = upstream_of(
         table, counts, cot, weights[0], acts, norm_gain, feature_blocks, capacity
     )
     other_stats = flipped(own_stats, "tensor", 1)
     term, first_sent, mine, theirs = terms_of(
-        core, scaled, acts, norm_gain, own_stats, other_stats, half_width * tensor_size
+        core, scaled, local_acts, local_gain, own_stats, other_stats, half_width * tensor_size
     )
     section = lax.axis_index("section")[None]
     arrived = relay(term, first_sent, section, "section")

time: 88.3 us -> 86.1 us (0.975)
  starting transfers between devices: 18.4 us -> 17.2 us
    ppermute x4, starting transfers between devices: 5.29 us -> 4.06 us  [relay(): arrived.append(lax.ppermute(sent, axis, pairs))]
    unnamed x22 -> x20, local copies, waits for them, and re-layouts: 2.88 us -> 2.87 us
  transfers between devices with their start and end apart: 17 -> 17, of which waited for: 7 -> 6; matrix products, arithmetic and copies ran while one was open for 0% -> 0% of each run, Pallas kernels for 22% -> 22%
where the time goes in v2:
time: 86.1 us; the launch traced here: 85.7 us
  waiting for transfers between devices  38.1 us (44%)
  Pallas kernels  26.7 us (31%)
  starting transfers between devices  17.2 us (20%)
  local copies, waits for them, and re-layouts  2.87 us (3%)
    ppermute x4, waiting for transfers between devices, relay(): arrived.append(lax.ppermute(sent, axis, pairs))  25 us
    ppermute x13, starting transfers between devices, flipped(): return lax.ppermute(value, axis, [(k, k ^ bit) for k in range(count)])  13.2 us
    ppermute x13, waiting for transfers between devices, flipped(): return lax.ppermute(value, axis, [(k, k ^ bit) for k in range(count)])  13.1 us
    pallas_call x2, Pallas kernels, precondition(): pl.pallas_call(functools.partial(feature_kernel, pieces=pieces, place=pla...  12.1 us
    pallas_call x1, Pallas kernels, invert_value(): pl.pallas_call(functools.partial(value_kernel, pieces=len(pieces)), in_sp...  4.47 us
    pallas_call x1, Pallas kernels, upstream_of(): pl.pallas_call(functools.partial(upstream_kernel, position=position, capa...  4.24 us
    ppermute x4, starting transfers between devices, relay(): arrived.append(lax.ppermute(sent, axis, pairs))  4.06 us
    pallas_call x1, Pallas kernels, place_rows(): pl.pallas_call(functools.partial(place_kernel, blocks=blocks), in_specs=[...  3.58 us
  transfers between devices with their start and end apart: 17, of which 6 were waited for; matrix products, arithmetic and copies ran while one was open for 0% of the time, Pallas kernels for 22%

profile of v2, /device:TPU:0, one launch (start us, length us, event | category | flops | bytes accessed | tf_op | source)
XLA Modules:
  0.0 85.7 jit_solution(12503569940383039509)
XLA Ops:
  0.6 3.0 %collective-permute-start.9 = (bf16[128,1024]{1,0:T(8,128)(2,1)}, bf16[128,1024]{1,0:T(8,128)(2,1)S(1)}, u32[]{:S(2)}, u32[]{:S(2)}) collective-permute-start(bf16[128,1024]{1,0:T(8,128)(2,1)} %bitcast.10), channel_id=1, source_target_pairs={{0,4},{2,6},{4,0},{6,2},{1,5},{3,7},{5,1},{7,3},{8,12},{10,14},{12... | collective-permute-start | bytes 786440 | tf_op jit(solution)/shard_map/ppermute | solution.py:23
  3.7 6.5 %collective-permute-done.9.refs_2_.refs_6_ = bf16[128,1024]{1,0:T(8,128)(2,1)S(1)} collective-permute-done((bf16[128,1024]{1,0:T(8,128)(2,1)}, bf16[128,1024]{1,0:T(8,128)(2,1)S(1)}, u32[]{:S(2)}, u32[]{:S(2)}) %collective-permute-start.9) | collective-permute-done | bytes 262176 | tf_op jit(solution)/shard_map/ppermute | solution.py:23
  10.2 4.2 %upstream.1 = (f32[128,2048]{1,0:T(8,128)S(1)}, f32[8,128]{1,0:T(8,128)S(1)}, bf16[128,2048]{1,0:T(8,128)(2,1)S(1)}, f32[1,2048]{1,0:T(1,128)S(1)}) custom-call(s32[13]{0:T(128)} %bitcast.20, s32[4]{0:T(128)} %bitcast.23, bf16[128,1024]{1,0:T(8,128)(2,1)} %bitcast.12, bf16[2048,1024]{1,0:T(8,128)(2,1)} %bitcast.16, bf16[128,2048]{1,0:T(8,128)(2,1)} %bitcast.19, ...), custom_call_target="tpu_custom_call" | custom-call | flops 536870912 | bytes 6291456 | tf_op jit(solution)/shard_map/upstream/pallas_call | solution.py:140
  14.4 1.8 %collective-permute-start = (f32[8,128]{1,0:T(8,128)S(1)}, f32[8,128]{1,0:T(8,128)S(1)}, u32[]{:S(2)}, u32[]{:S(2)}) collective-permute-start(f32[8,128]{1,0:T(8,128)S(1)} %get-tuple-element.15.own_ref.own_stats), channel_id=1, source_target_pairs={{0,1},{1,0},{2,3},{3,2},{4,5},{5,4},{6,7},{7,6},{8,9},{9,8},{10,11... | collective-permute-start | bytes 12296 | tf_op jit(solution)/shard_map/ppermute | solution.py:23
  16.3 1.8 %collective-permute-done.other_ref.other_stats = f32[8,128]{1,0:T(8,128)S(1)} collective-permute-done((f32[8,128]{1,0:T(8,128)S(1)}, f32[8,128]{1,0:T(8,128)S(1)}, u32[]{:S(2)}, u32[]{:S(2)}) %collective-permute-start) | collective-permute-done | bytes 4128 | tf_op jit(solution)/shard_map/ppermute | solution.py:23
  18.2 4.5 %value_inverse.1.refs_8_ = bf16[512,512]{1,0:T(8,128)(2,1)S(1)} custom-call(s32[1]{0:T(128)} %bitcast.1.core, s32[1]{0:T(128)} %bitcast.8.tensor, f32[8,128]{1,0:T(8,128)S(1)} %get-tuple-element.15.own_ref.own_stats, f32[8,128]{1,0:T(8,128)S(1)} %collective-permute-done.other_ref.other_stats, bf16[128,1024]{1,0:T(8,128)(2,1)S(1)} %bitcast.13, ...), custom_call_target="tpu_custom_call" | custom-call | flops 2952790016 | bytes 1048576 | tf_op jit(solution)/shard_map/value_inverse/pallas_call | solution.py:301
  22.6 0.1 collective-permute-start.11
  22.7 1.0 %terms.1 = (bf16[128,2048]{1,0:T(8,128)(2,1)S(1)}, bf16[128,512]{1,0:T(8,128)(2,1)S(1)}, bf16[128,512]{1,0:T(8,128)(2,1)S(1)}, bf16[128,512]{1,0:T(8,128)(2,1)S(...) custom-call(s32[1]{0:T(128)} %bitcast.1.core, f32[128,2048]{1,0:T(8,128)S(1)} %get-tuple-element.12.scaled_ref, ...), custom_call_target="tpu_custom_call" | custom-call | flops 2097152 | bytes 2621440 | tf_op jit(solution)/shard_map/terms/pallas_call | solution.py:195
  23.7 1.7 %collective-permute-start.6 = (bf16[128,512]{1,0:T(8,128)(2,1)S(1)}, bf16[128,512]{1,0:T(8,128)(2,1)S(1)}, u32[]{:S(2)}, u32[]{:S(2)}) collective-permute-start(bf16[128,512]{1,0:T(8,128)(2,1)S(1)} %get-tuple-element.18.refs_0_), channel_id=1, source_target_pairs={{0,4},{2,6},{4,0},{6,2},{1,5},{3,7},{5,1},{7,3},{8,12},{10,14},{12... | collective-permute-start | bytes 393224 | tf_op jit(solution)/shard_map/ppermute | solution.py:23
  25.5 0.1 collective-permute-start.7
  25.6 0.3 collective-permute-start.5
  25.9 1.6 %collective-permute-start.14 = (bf16[128,512]{1,0:T(8,128)(2,1)S(1)}, bf16[128,512]{1,0:T(8,128)(2,1)S(1)}, u32[]{:S(2)}, u32[]{:S(2)}) collective-permute-start(bf16[128,512]{1,0:T(8,128)(2,1)S(1)} %get-tuple-element.21), channel_id=1, source_target_pairs={{0,6},{2,4},{4,2},{6,0},{1,7},{3,5},{5,3},{7,1},{8,14},{10,12},{12... | collective-permute-start | bytes 393224 | tf_op jit(solution)/shard_map/ppermute | solution.py:23
  27.4 2.7 %collective-permute-done.6.refs_2_ = bf16[128,512]{1,0:T(8,128)(2,1)S(1)} collective-permute-done((bf16[128,512]{1,0:T(8,128)(2,1)S(1)}, bf16[128,512]{1,0:T(8,128)(2,1)S(1)}, u32[]{:S(2)}, u32[]{:S(2)}) %collective-permute-start.6) | collective-permute-done | bytes 131104 | tf_op jit(solution)/shard_map/ppermute | solution.py:23
  30.1 2.1 %collective-permute-done.7.refs_3_ = bf16[128,512]{1,0:T(8,128)(2,1)S(1)} collective-permute-done((bf16[128,512]{1,0:T(8,128)(2,1)S(1)}, bf16[128,512]{1,0:T(8,128)(2,1)S(1)}, u32[]{:S(2)}, u32[]{:S(2)}) %collective-permute-start.7) | collective-permute-done | bytes 131104 | tf_op jit(solution)/shard_map/ppermute | solution.py:23
  32.2 1.5 %collective-permute-start.13 = (bf16[128,512]{1,0:T(8,128)(2,1)S(1)}, bf16[128,512]{1,0:T(8,128)(2,1)S(1)}, u32[]{:S(2)}, u32[]{:S(2)}) collective-permute-start(bf16[128,512]{1,0:T(8,128)(2,1)S(1)} %get-tuple-element.20.refs_0_), channel_id=1, source_target_pairs={{0,4},{2,6},{4,0},{6,2},{1,5},{3,7},{5,1},{7,3},{8,12},{10,14},{12... | collective-permute-start | bytes 393224 | tf_op jit(solution)/shard_map/ppermute | solution.py:23
  33.7 0.8 collective-permute-start.1
  34.5 0.9 %copy-done.8 = bf16[128,1024]{1,0:T(8,128)(2,1)S(1)} copy-done((bf16[128,1024]{1,0:T(8,128)(2,1)S(1)}, bf16[128,1024]{1,0:T(8,128)(2,1)}, u32[]{:S(2)}) %copy-start.8) | copy-done | bytes 262168
  35.5 4.9 %precondition.2.refs_0_ = bf16[512,1024]{1,0:T(8,128)(2,1)S(1)} custom-call(s32[1]{0:T(128)} %bitcast.1.core, s32[13]{0:T(128)} %bitcast.21, s32[4]{0:T(128)} %bitcast.24, bf16[128,512]{1,0:T(8,128)(2,1)S(1)} %get-tuple-element.18.refs_0_, bf16[128,512]{1,0:T(8,128)(2,1)S(1)} %collective-permute-done.5.refs_1_, ...), custom_call_target="tpu_custom_call" | custom-call | flops 4563402752 | bytes 2097152 | tf_op jit(solution)/shard_map/precondition/pallas_call | solution.py:333
  40.4 3.0 %collective-permute-start.15 = (bf16[512,1024]{1,0:T(8,128)(2,1)S(1)}, bf16[512,1024]{1,0:T(8,128)(2,1)S(1)}, u32[]{:S(2)}, u32[]{:S(2)}) collective-permute-start(bf16[512,1024]{1,0:T(8,128)(2,1)S(1)} %precondition.2.refs_0_), channel_id=1, source_target_pairs={{0,2},{2,0},{4,6},{6,4},{1,3},{3,1},{5,7},{7,5},{8,10},{10,8},{12,... | collective-permute-start | bytes 3145736 | tf_op jit(solution)/shard_map/ppermute | solution.py:23
  43.4 0.9 %copy-done.4 = bf16[128,1024]{1,0:T(8,128)(2,1)S(1)} copy-done((bf16[128,1024]{1,0:T(8,128)(2,1)S(1)}, bf16[128,1024]{1,0:T(8,128)(2,1)}, u32[]{:S(2)}) %copy-start.4) | copy-done | bytes 262168
  44.4 0.9 %copy-done.6 = bf16[128,1024]{1,0:T(8,128)(2,1)S(1)} copy-done((bf16[128,1024]{1,0:T(8,128)(2,1)S(1)}, bf16[128,1024]{1,0:T(8,128)(2,1)}, u32[]{:S(2)}) %copy-start.6) | copy-done | bytes 262168
  45.3 7.2 %precondition.3.refs_1_ = bf16[512,1024]{1,0:T(8,128)(2,1)} custom-call(s32[1]{0:T(128)} %bitcast.1.core, s32[13]{0:T(128)} %bitcast.22, s32[4]{0:T(128)} %bitcast.25, bf16[128,512]{1,0:T(8,128)(2,1)S(1)} %get-tuple-element.20.refs_0_, bf16[128,512]{1,0:T(8,128)(2,1)S(1)} %collective-permute-done.12.refs_1_, ...), custom_call_target="tpu_custom_call" | custom-call | flops 4563402752 | bytes 2097152 | tf_op jit(solution)/shard_map/precondition/pallas_call | solution.py:333
  52.6 0.1 payload.3
  52.6 0.7 collective-permute-start.2
  53.3 0.1 payload.4
  53.4 1.3 %collective-permute-start.3 = (bf16[64,2048]{1,0:T(8,128)(2,1)S(1)}, bf16[64,2048]{1,0:T(8,128)(2,1)S(1)}, u32[]{:S(2)}, u32[]{:S(2)}) collective-permute-start(bf16[64,2048]{1,0:T(8,128)(2,1)S(1)} %payload.4), channel_id=1, source_target_pairs={{8,0},{16,8},{9,1},{17,9},{10,2},{18,10},{11,3},{19,11},{12,4},{20... | collective-permute-start | bytes 786440 | tf_op jit(solution)/shard_map/ppermute | solution.py:246
  54.7 13.9 %collective-permute-done.3.arrived.refs_2_ = bf16[64,2048]{1,0:T(8,128)(2,1)S(1)} collective-permute-done((bf16[64,2048]{1,0:T(8,128)(2,1)S(1)}, bf16[64,2048]{1,0:T(8,128)(2,1)S(1)}, u32[]{:S(2)}, u32[]{:S(2)}) %collective-permute-start.3) | collective-permute-done | bytes 262176 | tf_op jit(solution)/shard_map/ppermute | solution.py:246
  68.6 0.1 payload.5
  68.7 1.3 %collective-permute-start.4 = (bf16[64,2048]{1,0:T(8,128)(2,1)S(1)}, bf16[64,2048]{1,0:T(8,128)(2,1)S(1)}, u32[]{:S(2)}, u32[]{:S(2)}) collective-permute-start(bf16[64,2048]{1,0:T(8,128)(2,1)S(1)} %payload.5), channel_id=1, source_target_pairs={{8,0},{9,1},{10,2},{11,3},{12,4},{13,5},{14,6},{15,7}} | collective-permute-start | bytes 786440 | tf_op jit(solution)/shard_map/ppermute | solution.py:246
  70.0 11.0 %collective-permute-done.4.refs_3_ = bf16[64,2048]{1,0:T(8,128)(2,1)S(1)} collective-permute-done((bf16[64,2048]{1,0:T(8,128)(2,1)S(1)}, bf16[64,2048]{1,0:T(8,128)(2,1)S(1)}, u32[]{:S(2)}, u32[]{:S(2)}) %collective-permute-start.4) | collective-permute-done | bytes 262176 | tf_op jit(solution)/shard_map/ppermute | solution.py:246
  81.0 1.1 %finish.1 = bf16[128,2048]{1,0:T(8,128)(2,1)} custom-call(s32[1]{0:T(128)} %bitcast.section, bf16[128,2048]{1,0:T(8,128)(2,1)S(1)} %copy-done, bf16[128,2048]{1,0:T(8,128)(2,1)S(1)} %get-tuple-element.16.term.term_ref, bf16[64,2048]{1,0:T(8,128)(2,1)S(1)} %collective-permute-done.1.arrived.refs_0_, ...), custom_call_target="tpu_custom_call" | custom-call | flops 524288 | bytes 2097152 | tf_op jit(solution)/shard_map/finish/pallas_call | solution.py:271
  82.1 3.6 %place_rows.1 = bf16[2048,1024]{1,0:T(8,128)(2,1)} custom-call(s32[1]{0:T(128)} %bitcast.1.core, bf16[512,1024]{1,0:T(8,128)(2,1)S(1)} %precondition.2.refs_0_, bf16[512,1024]{1,0:T(8,128)(2,1)} %precondition.3.refs_1_, bf16[512,1024]{1,0:T(8,128)(2,1)S(1)} %collective-permute-done.15.refs_2_, bf16[512,1024]{1,0:T(8,128)(2,1)} %collective-permute-done.16.refs_3_), custom_call_target="tpu_custom_call" | custom-call | bytes 8388608 | tf_op jit(solution)/shard_map/place_rows/pallas_call | solution.py:365
  (32 shorter events, 0.1 us)
Async XLA Ops:
  0.6 17.5 %copy-start.1 = (bf16[1,128,1024]{2,1,0:T(8,128)(2,1)S(1)}, bf16[1,128,1024]{2,1,0:T(8,128)(2,1)}, u32[]{:S(2)}) copy-start(bf16[1,128,1024]{2,1,0:T(8,128)(2,1)} %param.10) | copy-start | bytes 786436
  0.6 9.6 %collective-permute-start.9 = (bf16[128,1024]{1,0:T(8,128)(2,1)}, bf16[128,1024]{1,0:T(8,128)(2,1)S(1)}, u32[]{:S(2)}, u32[]{:S(2)}) collective-permute-start(bf16[128,1024]{1,0:T(8,128)(2,1)} %bitcast.10), channel_id=1, source_target_pairs={{0,4},{2,6},{4,0},{6,2},{1,5},{3,7},{5,1},{7,3},{8,12},{10,14},{12... | collective-permute-start | bytes 786440 | tf_op jit(solution)/shard_map/ppermute | solution.py:23
  3.7 14.4 %collective-permute-start.8 = (bf16[128,1024]{1,0:T(8,128)(2,1)}, bf16[128,1024]{1,0:T(8,128)(2,1)S(1)}, u32[]{:S(2)}, u32[]{:S(2)}) collective-permute-start(bf16[128,1024]{1,0:T(8,128)(2,1)} %bitcast.11), channel_id=1, source_target_pairs={{0,2},{2,0},{4,6},{6,4},{1,3},{3,1},{5,7},{7,5},{8,10},{10,8},{12,... | collective-permute-start | bytes 786440 | tf_op jit(solution)/shard_map/ppermute | solution.py:23
  10.2 24.3 %copy-start.3 = (bf16[128,1024]{1,0:T(8,128)(2,1)}, bf16[128,1024]{1,0:T(8,128)(2,1)S(1)}, u32[]{:S(2)}) copy-start(bf16[128,1024]{1,0:T(8,128)(2,1)S(1)} %collective-permute-done.9.refs_2_.refs_6_) | copy-start | bytes 786436
  10.2 7.9 %collective-permute-start.10 = (bf16[128,1024]{1,0:T(8,128)(2,1)S(1)}, bf16[128,1024]{1,0:T(8,128)(2,1)S(1)}, u32[]{:S(2)}, u32[]{:S(2)}) collective-permute-start(bf16[128,1024]{1,0:T(8,128)(2,1)S(1)} %collective-permute-done.9.refs_2_.refs_6_), channel_id=1, source_target_pairs={{0,2},{2,0},{4,6},{6,4},{1,3},{3,1},{5,7},{7,5},{8,10},{10,8},{12,... | collective-permute-start | bytes 786440 | tf_op jit(solution)/shard_map/ppermute | solution.py:23
  14.4 3.7 %collective-permute-start = (f32[8,128]{1,0:T(8,128)S(1)}, f32[8,128]{1,0:T(8,128)S(1)}, u32[]{:S(2)}, u32[]{:S(2)}) collective-permute-start(f32[8,128]{1,0:T(8,128)S(1)} %get-tuple-element.15.own_ref.own_stats), channel_id=1, source_target_pairs={{0,1},{1,0},{2,3},{3,2},{4,5},{5,4},{6,7},{7,6},{8,9},{9,8},{10,11... | collective-permute-start | bytes 12296 | tf_op jit(solution)/shard_map/ppermute | solution.py:23
  18.1 16.4 %copy-start.5 = (bf16[128,1024]{1,0:T(8,128)(2,1)}, bf16[128,1024]{1,0:T(8,128)(2,1)S(1)}, u32[]{:S(2)}) copy-start(bf16[128,1024]{1,0:T(8,128)(2,1)S(1)} %collective-permute-done.8.refs_1_.refs_5_) | copy-start | bytes 786436
  18.1 4.5 %copy-start.7 = (bf16[128,1024]{1,0:T(8,128)(2,1)}, bf16[128,1024]{1,0:T(8,128)(2,1)S(1)}, u32[]{:S(2)}) copy-start(bf16[128,1024]{1,0:T(8,128)(2,1)S(1)} %collective-permute-done.10.refs_3_.refs_7_) | copy-start | bytes 786436
  22.6 11.9 %collective-permute-start.11 = (bf16[512,512]{1,0:T(8,128)(2,1)S(1)}, bf16[512,512]{1,0:T(8,128)(2,1)S(1)}, u32[]{:S(2)}, u32[]{:S(2)}) collective-permute-start(bf16[512,512]{1,0:T(8,128)(2,1)S(1)} %value_inverse.1.refs_8_), channel_id=1, source_target_pairs={{0,2},{2,0},{4,6},{6,4},{1,3},{3,1},{5,7},{7,5},{8,10},{10,8},{12,... | collective-permute-start | bytes 1572872 | tf_op jit(solution)/shard_map/ppermute | solution.py:23
  23.7 6.4 %collective-permute-start.6 = (bf16[128,512]{1,0:T(8,128)(2,1)S(1)}, bf16[128,512]{1,0:T(8,128)(2,1)S(1)}, u32[]{:S(2)}, u32[]{:S(2)}) collective-permute-start(bf16[128,512]{1,0:T(8,128)(2,1)S(1)} %get-tuple-element.18.refs_0_), channel_id=1, source_target_pairs={{0,4},{2,6},{4,0},{6,2},{1,5},{3,7},{5,1},{7,3},{8,12},{10,14},{12... | collective-permute-start | bytes 393224 | tf_op jit(solution)/shard_map/ppermute | solution.py:23
  25.5 6.7 %collective-permute-start.7 = (bf16[128,512]{1,0:T(8,128)(2,1)S(1)}, bf16[128,512]{1,0:T(8,128)(2,1)S(1)}, u32[]{:S(2)}, u32[]{:S(2)}) collective-permute-start(bf16[128,512]{1,0:T(8,128)(2,1)S(1)} %get-tuple-element.19), channel_id=1, source_target_pairs={{0,6},{2,4},{4,2},{6,0},{1,7},{3,5},{5,3},{7,1},{8,14},{10,12},{12... | collective-permute-start | bytes 393224 | tf_op jit(solution)/shard_map/ppermute | solution.py:23
  25.6 8.1 %collective-permute-start.5 = (bf16[128,512]{1,0:T(8,128)(2,1)S(1)}, bf16[128,512]{1,0:T(8,128)(2,1)S(1)}, u32[]{:S(2)}, u32[]{:S(2)}) collective-permute-start(bf16[128,512]{1,0:T(8,128)(2,1)S(1)} %get-tuple-element.19), channel_id=1, source_target_pairs={{0,2},{2,0},{4,6},{6,4},{1,3},{3,1},{5,7},{7,5},{8,10},{10,8},{12,... | collective-permute-start | bytes 393224 | tf_op jit(solution)/shard_map/ppermute | solution.py:23
  25.9 17.5 %collective-permute-start.14 = (bf16[128,512]{1,0:T(8,128)(2,1)S(1)}, bf16[128,512]{1,0:T(8,128)(2,1)S(1)}, u32[]{:S(2)}, u32[]{:S(2)}) collective-permute-start(bf16[128,512]{1,0:T(8,128)(2,1)S(1)} %get-tuple-element.21), channel_id=1, source_target_pairs={{0,6},{2,4},{4,2},{6,0},{1,7},{3,5},{5,3},{7,1},{8,14},{10,12},{12... | collective-permute-start | bytes 393224 | tf_op jit(solution)/shard_map/ppermute | solution.py:23
  30.1 13.3 %collective-permute-start.12 = (bf16[128,512]{1,0:T(8,128)(2,1)S(1)}, bf16[128,512]{1,0:T(8,128)(2,1)S(1)}, u32[]{:S(2)}, u32[]{:S(2)}) collective-permute-start(bf16[128,512]{1,0:T(8,128)(2,1)S(1)} %get-tuple-element.21), channel_id=1, source_target_pairs={{0,2},{2,0},{4,6},{6,4},{1,3},{3,1},{5,7},{7,5},{8,10},{10,8},{12,... | collective-permute-start | bytes 393224 | tf_op jit(solution)/shard_map/ppermute | solution.py:23
  32.2 11.2 %collective-permute-start.13 = (bf16[128,512]{1,0:T(8,128)(2,1)S(1)}, bf16[128,512]{1,0:T(8,128)(2,1)S(1)}, u32[]{:S(2)}, u32[]{:S(2)}) collective-permute-start(bf16[128,512]{1,0:T(8,128)(2,1)S(1)} %get-tuple-element.20.refs_0_), channel_id=1, source_target_pairs={{0,4},{2,6},{4,0},{6,2},{1,5},{3,7},{5,1},{7,3},{8,12},{10,14},{12... | collective-permute-start | bytes 393224 | tf_op jit(solution)/shard_map/ppermute | solution.py:23
  33.7 9.7 %copy-start.2 = (bf16[1,128,1024]{2,1,0:T(8,128)(2,1)S(1)}, bf16[1,128,1024]{2,1,0:T(8,128)(2,1)}, u32[]{:S(2)}) copy-start(bf16[1,128,1024]{2,1,0:T(8,128)(2,1)} %param.10) | copy-start | bytes 786436
  33.7 18.9 %collective-permute-start.1 = (bf16[64,2048]{1,0:T(8,128)(2,1)}, bf16[64,2048]{1,0:T(8,128)(2,1)S(1)}, u32[]{:S(2)}, u32[]{:S(2)}) collective-permute-start(bf16[64,2048]{1,0:T(8,128)(2,1)} %get-tuple-element.17), channel_id=1, source_target_pairs={{24,16},{25,17},{26,18},{27,19},{28,20},{29,21},{30,22},{31,23}} | collective-permute-start | bytes 786440 | tf_op jit(solution)/shard_map/ppermute | solution.py:246
  34.5 1.0 %copy-start.8 = (bf16[128,1024]{1,0:T(8,128)(2,1)S(1)}, bf16[128,1024]{1,0:T(8,128)(2,1)}, u32[]{:S(2)}) copy-start(bf16[128,1024]{1,0:T(8,128)(2,1)} %copy-done.7) | copy-start | bytes 786436
  35.5 7.9 %copy-start.9 = (bf16[128,1024]{1,0:T(8,128)(2,1)S(1)}, bf16[128,1024]{1,0:T(8,128)(2,1)}, u32[]{:S(2)}) copy-start(bf16[128,1024]{1,0:T(8,128)(2,1)} %copy-done.7) | copy-start | bytes 786436
  40.4 40.6 %copy-start = (bf16[128,2048]{1,0:T(8,128)(2,1)S(1)}, bf16[128,2048]{1,0:T(8,128)(2,1)}, u32[]{:S(2)}) copy-start(bf16[128,2048]{1,0:T(8,128)(2,1)} %top_ref.1) | copy-start | bytes 1572868
  40.4 41.7 %collective-permute-start.15 = (bf16[512,1024]{1,0:T(8,128)(2,1)S(1)}, bf16[512,1024]{1,0:T(8,128)(2,1)S(1)}, u32[]{:S(2)}, u32[]{:S(2)}) collective-permute-start(bf16[512,1024]{1,0:T(8,128)(2,1)S(1)} %precondition.2.refs_0_), channel_id=1, source_target_pairs={{0,2},{2,0},{4,6},{6,4},{1,3},{3,1},{5,7},{7,5},{8,10},{10,8},{12,... | collective-permute-start | bytes 3145736 | tf_op jit(solution)/shard_map/ppermute | solution.py:23
  43.4 1.0 %copy-start.4 = (bf16[128,1024]{1,0:T(8,128)(2,1)S(1)}, bf16[128,1024]{1,0:T(8,128)(2,1)}, u32[]{:S(2)}) copy-start(bf16[128,1024]{1,0:T(8,128)(2,1)} %copy-done.3) | copy-start | bytes 786436
  44.4 0.9 %copy-start.6 = (bf16[128,1024]{1,0:T(8,128)(2,1)S(1)}, bf16[128,1024]{1,0:T(8,128)(2,1)}, u32[]{:S(2)}) copy-start(bf16[128,1024]{1,0:T(8,128)(2,1)} %copy-done.5) | copy-start | bytes 786436
  52.6 29.6 %collective-permute-start.16 = (bf16[512,1024]{1,0:T(8,128)(2,1)}, bf16[512,1024]{1,0:T(8,128)(2,1)}, u32[]{:S(2)}, u32[]{:S(2)}) collective-permute-start(bf16[512,1024]{1,0:T(8,128)(2,1)} %precondition.3.refs_1_), channel_id=1, source_target_pairs={{0,2},{2,0},{4,6},{6,4},{1,3},{3,1},{5,7},{7,5},{8,10},{10,8},{12,... | collective-permute-start | bytes 3145736 | tf_op jit(solution)/shard_map/ppermute | solution.py:23
  52.6 0.7 collective-permute-start.2
  53.4 15.2 %collective-permute-start.3 = (bf16[64,2048]{1,0:T(8,128)(2,1)S(1)}, bf16[64,2048]{1,0:T(8,128)(2,1)S(1)}, u32[]{:S(2)}, u32[]{:S(2)}) collective-permute-start(bf16[64,2048]{1,0:T(8,128)(2,1)S(1)} %payload.4), channel_id=1, source_target_pairs={{8,0},{16,8},{9,1},{17,9},{10,2},{18,10},{11,3},{19,11},{12,4},{20... | collective-permute-start | bytes 786440 | tf_op jit(solution)/shard_map/ppermute | solution.py:246
  68.7 12.3 %collective-permute-start.4 = (bf16[64,2048]{1,0:T(8,128)(2,1)S(1)}, bf16[64,2048]{1,0:T(8,128)(2,1)S(1)}, u32[]{:S(2)}, u32[]{:S(2)}) collective-permute-start(bf16[64,2048]{1,0:T(8,128)(2,1)S(1)} %payload.5), channel_id=1, source_target_pairs={{8,0},{9,1},{10,2},{11,3},{12,4},{13,5},{14,6},{15,7}} | collective-permute-start | bytes 786440 | tf_op jit(solution)/shard_map/ppermute | solution.py:246

commit v3 on v2

--- a/solution.py
+++ b/solution.py
@@ -14,7 +14,6 @@
 LANES = 128
 STAT_ROWS = 8
 RELAY_CHUNKS = 2
-RELAY_LAG = 1
 VMEM_LIMIT = 24 * 2**20
 
 
@@ -167,7 +166,7 @@
 
 
 def terms_kernel(core, scaled_ref, act_ref, gain_ref, own_ref, other_ref, term_ref, *refs, full_width):
-    normed, first_sent, pieces = refs[-1], refs[-2], refs[:-2]
+    normed, chunks, pieces = refs[-1], refs[-1 - RELAY_CHUNKS : -1], refs[: -1 - RELAY_CHUNKS]
     squares = own_ref[0:1] + other_ref[0:1]
     inner_sum = own_ref[1:2] + other_ref[1:2]
     inverse_rms = lax.rsqrt(squares * (1.0 / full_width) + EPSILON)
@@ -177,7 +176,9 @@
     normed[...] = (inputs * inverse_rms * gain_ref[...]).astype(jnp.bfloat16)
     term = inverse_rms * scaled_ref[...] - inputs * coefficient
     term_ref[...] = term.astype(jnp.bfloat16)
-    first_sent[...] = term[: first_sent.shape[0]].astype(jnp.bfloat16)
+    for k, chunk in enumerate(chunks):
+        rows = chunk.shape[0]
+        chunk[...] = term[k * rows : (k + 1) * rows].astype(jnp.bfloat16)
     half = normed.shape[1] // 2
     blocks = half // BLOCK
     for k in range(blocks):
@@ -195,10 +196,10 @@
     outs = pl.pallas_call(
         functools.partial(terms_kernel, full_width=full_width),
         in_specs=[smem] + [vmem] * 5,
-        out_specs=[vmem] * (2 + blocks),
+        out_specs=[vmem] * (1 + blocks + RELAY_CHUNKS),
         out_shape=[jax.ShapeDtypeStruct((tokens, width), jnp.bfloat16)]
         + [jax.ShapeDtypeStruct((tokens, BLOCK), jnp.bfloat16)] * blocks
-        + [jax.ShapeDtypeStruct((tokens // RELAY_CHUNKS, width), jnp.bfloat16)],
+        + [jax.ShapeDtypeStruct((tokens // RELAY_CHUNKS, width), jnp.bfloat16)] * RELAY_CHUNKS,
         scratch_shapes=[pltpu.VMEM((tokens, width), jnp.bfloat16)],
         compiler_params=pltpu.CompilerParams(vmem_limit_bytes=VMEM_LIMIT),
         cost_estimate=pl.CostEstimate(
@@ -206,49 +207,53 @@
         ),
         name="terms",
     )(core, *in_vmem(scaled, activations, gain, own_stats, other_stats))
-    return outs[0], outs[-1], outs[1 : 1 + blocks // 2], outs[1 + blocks // 2 : -1]
-
-
-def payload_kernel(section, term, arrived, out, *, wave, sections):
+    split = 1 + blocks // 2
+    return outs[0], outs[-RELAY_CHUNKS:], outs[1:split], outs[split:-RELAY_CHUNKS]
+
+
+def payload_kernel(section, term, *refs, wave, sections):
+    arrived, out = refs[:-1], refs[-1]
     rows = out.shape[0]
-    chunk = wave - RELAY_LAG * (sections - 1 - section[0])
-    chunk = jnp.minimum(jnp.maximum(chunk, 0), RELAY_CHUNKS - 1)
-    own = term[pl.ds(pl.multiple_of(chunk * rows, rows), rows)].astype(jnp.float32)
-    out[...] = (own + arrived[...].astype(jnp.float32)).astype(jnp.bfloat16)
+    chunk = jnp.minimum(jnp.maximum(wave - (sections - 1 - section[0]), 0), RELAY_CHUNKS - 1)
+    total = term[pl.ds(pl.multiple_of(chunk * rows, rows), rows)].astype(jnp.float32)
+    for part in arrived:
+        total = total + part[...].astype(jnp.float32)
+    out[...] = total.astype(jnp.bfloat16)
 
 
 def payload(section, term, arrived, wave, sections):
     return pl.pallas_call(
         functools.partial(payload_kernel, wave=wave, sections=sections),
-        in_specs=[SMEM, VMEM, VMEM],
+        in_specs=[SMEM] + [VMEM] * (1 + len(arrived)),
         out_specs=VMEM,
-        out_shape=jax.ShapeDtypeStruct(arrived.shape, jnp.bfloat16),
-        compiler_params=pltpu.CompilerParams(vmem_limit_bytes=VMEM_LIMIT),
-        cost_estimate=pl.CostEstimate(
-            flops=arrived.size, bytes_accessed=6 * arrived.size, transcendentals=0
+        out_shape=jax.ShapeDtypeStruct(arrived[0].shape, jnp.bfloat16),
+        compiler_params=pltpu.CompilerParams(vmem_limit_bytes=VMEM_LIMIT),
+        cost_estimate=pl.CostEstimate(
+            flops=term.size, bytes_accessed=4 * term.size, transcendentals=0
         ),
         name="payload",
-    )(section, *in_vmem(term, arrived))
-
-
-def relay(term, first_sent, section, axis):
+    )(section, *in_vmem(term, *arrived))
+
+
+def relay(term, chunks, section, axis):
     count = lax.axis_size(axis)
-    arrived = []
-    for wave in range(RELAY_CHUNKS + RELAY_LAG * (count - 2)):
-        sent = first_sent
-        if wave >= RELAY_LAG:
-            sent = payload(section, term, arrived[wave - RELAY_LAG], wave, count)
-        pairs = [
-            (k, k - 1)
-            for k in range(1, count)
-            if 0 <= wave - RELAY_LAG * (count - 1 - k) < RELAY_CHUNKS
-        ]
+    last = count - 1
+    early = []
+    for chunk in chunks:
+        early.append(lax.ppermute(chunk, axis, [(last, last - 1)]))
+    arrived = [None]
+    for wave in range(1, RELAY_CHUNKS + count - 2):
+        parts = [early[wave - 1]] if wave <= RELAY_CHUNKS else []
+        if wave >= 2:
+            parts.append(arrived[wave - 1])
+        sent = payload(section, term, parts, wave, count)
+        pairs = [(k, k - 1) for k in range(1, last) if 0 <= wave - (last - k) < RELAY_CHUNKS]
         arrived.append(lax.ppermute(sent, axis, pairs))
-    return arrived
+    return early, arrived[1:]
 
 
 def finish_kernel(section, top_ref, term_ref, *refs, sections):
-    arrived, out = refs[:-1], refs[-1]
+    early, arrived, out = refs[:RELAY_CHUNKS], refs[RELAY_CHUNKS:-1], refs[-1]
     rows = arrived[0].shape[0]
     for chunk in range(RELAY_CHUNKS):
         span = slice(chunk * rows, (chunk + 1) * rows)
@@ -259,7 +264,8 @@
             out[span] = own.astype(jnp.bfloat16)
 
         for place in range(sections - 1):
-            later = arrived[chunk + RELAY_LAG * (sections - 2 - place)]
+            hops = sections - 2 - place
+            later = arrived[chunk + hops - 1] if hops else early[chunk]
 
             @pl.when(section[0] == place)
             def _(span=span, own=own, later=later):
@@ -401,11 +407,11 @@
         table, counts, cot, weights[0], acts, norm_gain, feature_blocks, capacity
     )
     other_stats = flipped(own_stats, "tensor", 1)
-    term, first_sent, mine, theirs = terms_of(
+    term, chunks, mine, theirs = terms_of(
         core, scaled, local_acts, local_gain, own_stats, other_stats, half_width * tensor_size
     )
     section = lax.axis_index("section")[None]
-    arrived = relay(term, first_sent, section, "section")
+    early, arrived = relay(term, chunks, section, "section")
 
     normed = []
     for own, sent in zip(mine, theirs):
@@ -427,7 +433,7 @@
         )
         received.append(flipped(own_rows[k], "dp", 1))
     output = place_rows(core, own_rows, received)
-    input_grad = finish(section, lax.axis_size("section"), top_grad, term, arrived)
+    input_grad = finish(section, lax.axis_size("section"), top_grad, term, early + arrived)
     return (input_grad[None], output[None])
 
 

time: 86.1 us -> 86.2 us (level)
    ppermute x0 -> x2, starting transfers between devices: none -> 1.47 us  [relay(): early.append(lax.ppermute(chunk, axis, [(last, last - 1)]))]
    ppermute x4 -> x3, starting transfers between devices: 4.06 us -> 3.26 us  [relay(): arrived.append(lax.ppermute(sent, axis, pairs))]
    ppermute x4 -> x3, waiting for transfers between devices: 25 us -> 24.4 us  [relay(): arrived.append(lax.ppermute(sent, axis, pairs))]
    unnamed x20 -> x22, local copies, waits for them, and re-layouts: 2.87 us -> 2.87 us
  transfers between devices with their start and end apart: 17 -> 18, of which waited for: 6 -> 6; matrix products, arithmetic and copies ran while one was open for 0% -> 0% of each run, Pallas kernels for 22% -> 22%
where the time goes in v3:
time: 86.2 us; the launch traced here: 85.9 us
  waiting for transfers between devices  37.5 us (44%)
  Pallas kernels  26.8 us (31%)
  starting transfers between devices  17.9 us (21%)
  local copies, waits for them, and re-layouts  2.87 us (3%)
    ppermute x3, waiting for transfers between devices, relay(): arrived.append(lax.ppermute(sent, axis, pairs))  24.4 us
    ppermute x13, starting transfers between devices, flipped(): return lax.ppermute(value, axis, [(k, k ^ bit) for k in range(count)])  13.2 us
    ppermute x13, waiting for transfers between devices, flipped(): return lax.ppermute(value, axis, [(k, k ^ bit) for k in range(count)])  13.1 us
    pallas_call x2, Pallas kernels, precondition(): pl.pallas_call(functools.partial(feature_kernel, pieces=pieces, place=pla...  12.1 us
    pallas_call x1, Pallas kernels, invert_value(): pl.pallas_call(functools.partial(value_kernel, pieces=len(pieces)), in_sp...  4.47 us
    pallas_call x1, Pallas kernels, upstream_of(): pl.pallas_call(functools.partial(upstream_kernel, position=position, capa...  4.24 us
    pallas_call x1, Pallas kernels, place_rows(): pl.pallas_call(functools.partial(place_kernel, blocks=blocks), in_specs=[...  3.58 us
    ppermute x3, starting transfers between devices, relay(): arrived.append(lax.ppermute(sent, axis, pairs))  3.26 us
  transfers between devices with their start and end apart: 18, of which 6 were waited for; matrix products, arithmetic and copies ran while one was open for 0% of the time, Pallas kernels for 22%

profile of v3, /device:TPU:0, one launch (start us, length us, event | category | flops | bytes accessed | tf_op | source)
XLA Modules:
  0.0 85.9 jit_solution(11419053778234201587)
XLA Ops:
  0.6 3.0 %collective-permute-start.10 = (bf16[128,1024]{1,0:T(8,128)(2,1)}, bf16[128,1024]{1,0:T(8,128)(2,1)S(1)}, u32[]{:S(2)}, u32[]{:S(2)}) collective-permute-start(bf16[128,1024]{1,0:T(8,128)(2,1)} %bitcast.10), channel_id=1, source_target_pairs={{0,4},{2,6},{4,0},{6,2},{1,5},{3,7},{5,1},{7,3},{8,12},{10,14},{12... | collective-permute-start | bytes 786440 | tf_op jit(solution)/shard_map/ppermute | solution.py:22
  3.7 6.5 %collective-permute-done.10.refs_2_.refs_6_ = bf16[128,1024]{1,0:T(8,128)(2,1)S(1)} collective-permute-done((bf16[128,1024]{1,0:T(8,128)(2,1)}, bf16[128,1024]{1,0:T(8,128)(2,1)S(1)}, u32[]{:S(2)}, u32[]{:S(2)}) %collective-permute-start.10) | collective-permute-done | bytes 262176 | tf_op jit(solution)/shard_map/ppermute | solution.py:22
  10.2 4.2 %upstream.1 = (f32[128,2048]{1,0:T(8,128)S(1)}, f32[8,128]{1,0:T(8,128)S(1)}, bf16[128,2048]{1,0:T(8,128)(2,1)S(1)}, f32[1,2048]{1,0:T(1,128)S(1)}) custom-call(s32[13]{0:T(128)} %bitcast.20, s32[4]{0:T(128)} %bitcast.23, bf16[128,1024]{1,0:T(8,128)(2,1)} %bitcast.12, bf16[2048,1024]{1,0:T(8,128)(2,1)} %bitcast.16, bf16[128,2048]{1,0:T(8,128)(2,1)} %bitcast.19, ...), custom_call_target="tpu_custom_call" | custom-call | flops 536870912 | bytes 6291456 | tf_op jit(solution)/shard_map/upstream/pallas_call | solution.py:139
  14.4 1.8 %collective-permute-start = (f32[8,128]{1,0:T(8,128)S(1)}, f32[8,128]{1,0:T(8,128)S(1)}, u32[]{:S(2)}, u32[]{:S(2)}) collective-permute-start(f32[8,128]{1,0:T(8,128)S(1)} %get-tuple-element.16.own_ref.own_stats), channel_id=1, source_target_pairs={{0,1},{1,0},{2,3},{3,2},{4,5},{5,4},{6,7},{7,6},{8,9},{9,8},{10,11... | collective-permute-start | bytes 12296 | tf_op jit(solution)/shard_map/ppermute | solution.py:22
  16.3 1.8 %collective-permute-done.other_ref.other_stats = f32[8,128]{1,0:T(8,128)S(1)} collective-permute-done((f32[8,128]{1,0:T(8,128)S(1)}, f32[8,128]{1,0:T(8,128)S(1)}, u32[]{:S(2)}, u32[]{:S(2)}) %collective-permute-start) | collective-permute-done | bytes 4128 | tf_op jit(solution)/shard_map/ppermute | solution.py:22
  18.1 4.5 %value_inverse.1.refs_8_ = bf16[512,512]{1,0:T(8,128)(2,1)S(1)} custom-call(s32[1]{0:T(128)} %bitcast.1.core, s32[1]{0:T(128)} %bitcast.8.tensor, f32[8,128]{1,0:T(8,128)S(1)} %get-tuple-element.16.own_ref.own_stats, f32[8,128]{1,0:T(8,128)S(1)} %collective-permute-done.other_ref.other_stats, bf16[128,1024]{1,0:T(8,128)(2,1)S(1)} %bitcast.13, ...), custom_call_target="tpu_custom_call" | custom-call | flops 2952790016 | bytes 1048576 | tf_op jit(solution)/shard_map/value_inverse/pallas_call | solution.py:307
  22.6 0.1 collective-permute-start.12
  22.7 1.0 %terms.1 = (bf16[128,2048]{1,0:T(8,128)(2,1)S(1)}, bf16[128,512]{1,0:T(8,128)(2,1)S(1)}, bf16[128,512]{1,0:T(8,128)(2,1)S(1)}, bf16[128,512]{1,0:T(8,128)(2,1)S(...) custom-call(s32[1]{0:T(128)} %bitcast.1.core, ...), custom_call_target="tpu_custom_call" | custom-call | flops 2097152 | bytes 2621440 | tf_op jit(solution)/shard_map/terms/pallas_call | solution.py:196
  23.7 1.8 %collective-permute-start.7 = (bf16[128,512]{1,0:T(8,128)(2,1)S(1)}, bf16[128,512]{1,0:T(8,128)(2,1)S(1)}, u32[]{:S(2)}, u32[]{:S(2)}) collective-permute-start(bf16[128,512]{1,0:T(8,128)(2,1)S(1)} %get-tuple-element.20.refs_0_), channel_id=1, source_target_pairs={{0,4},{2,6},{4,0},{6,2},{1,5},{3,7},{5,1},{7,3},{8,12},{10,14},{12... | collective-permute-start | bytes 393224 | tf_op jit(solution)/shard_map/ppermute | solution.py:22
  25.5 0.1 collective-permute-start.8
  25.6 0.3 collective-permute-start.6
  25.9 1.6 %collective-permute-start.15 = (bf16[128,512]{1,0:T(8,128)(2,1)S(1)}, bf16[128,512]{1,0:T(8,128)(2,1)S(1)}, u32[]{:S(2)}, u32[]{:S(2)}) collective-permute-start(bf16[128,512]{1,0:T(8,128)(2,1)S(1)} %get-tuple-element.23), channel_id=1, source_target_pairs={{0,6},{2,4},{4,2},{6,0},{1,7},{3,5},{5,3},{7,1},{8,14},{10,12},{12... | collective-permute-start | bytes 393224 | tf_op jit(solution)/shard_map/ppermute | solution.py:22
  27.4 2.7 %collective-permute-done.7.refs_2_ = bf16[128,512]{1,0:T(8,128)(2,1)S(1)} collective-permute-done((bf16[128,512]{1,0:T(8,128)(2,1)S(1)}, bf16[128,512]{1,0:T(8,128)(2,1)S(1)}, u32[]{:S(2)}, u32[]{:S(2)}) %collective-permute-start.7) | collective-permute-done | bytes 131104 | tf_op jit(solution)/shard_map/ppermute | solution.py:22
  30.1 2.1 %collective-permute-done.8.refs_3_ = bf16[128,512]{1,0:T(8,128)(2,1)S(1)} collective-permute-done((bf16[128,512]{1,0:T(8,128)(2,1)S(1)}, bf16[128,512]{1,0:T(8,128)(2,1)S(1)}, u32[]{:S(2)}, u32[]{:S(2)}) %collective-permute-start.8) | collective-permute-done | bytes 131104 | tf_op jit(solution)/shard_map/ppermute | solution.py:22
  32.2 1.5 %collective-permute-start.14 = (bf16[128,512]{1,0:T(8,128)(2,1)S(1)}, bf16[128,512]{1,0:T(8,128)(2,1)S(1)}, u32[]{:S(2)}, u32[]{:S(2)}) collective-permute-start(bf16[128,512]{1,0:T(8,128)(2,1)S(1)} %get-tuple-element.22.refs_0_), channel_id=1, source_target_pairs={{0,4},{2,6},{4,0},{6,2},{1,5},{3,7},{5,1},{7,3},{8,12},{10,14},{12... | collective-permute-start | bytes 393224 | tf_op jit(solution)/shard_map/ppermute | solution.py:22
  33.7 0.8 collective-permute-start.1
  34.5 0.9 %copy-done.8 = bf16[128,1024]{1,0:T(8,128)(2,1)S(1)} copy-done((bf16[128,1024]{1,0:T(8,128)(2,1)S(1)}, bf16[128,1024]{1,0:T(8,128)(2,1)}, u32[]{:S(2)}) %copy-start.8) | copy-done | bytes 262168
  35.5 4.9 %precondition.2.refs_0_ = bf16[512,1024]{1,0:T(8,128)(2,1)S(1)} custom-call(s32[1]{0:T(128)} %bitcast.1.core, s32[13]{0:T(128)} %bitcast.21, s32[4]{0:T(128)} %bitcast.24, bf16[128,512]{1,0:T(8,128)(2,1)S(1)} %get-tuple-element.20.refs_0_, bf16[128,512]{1,0:T(8,128)(2,1)S(1)} %collective-permute-done.6.refs_1_, ...), custom_call_target="tpu_custom_call" | custom-call | flops 4563402752 | bytes 2097152 | tf_op jit(solution)/shard_map/precondition/pallas_call | solution.py:339
  40.4 3.0 %collective-permute-start.16 = (bf16[512,1024]{1,0:T(8,128)(2,1)S(1)}, bf16[512,1024]{1,0:T(8,128)(2,1)S(1)}, u32[]{:S(2)}, u32[]{:S(2)}) collective-permute-start(bf16[512,1024]{1,0:T(8,128)(2,1)S(1)} %precondition.2.refs_0_), channel_id=1, source_target_pairs={{0,2},{2,0},{4,6},{6,4},{1,3},{3,1},{5,7},{7,5},{8,10},{10,8},{12,... | collective-permute-start | bytes 3145736 | tf_op jit(solution)/shard_map/ppermute | solution.py:22
  43.4 0.9 %copy-done.4 = bf16[128,1024]{1,0:T(8,128)(2,1)S(1)} copy-done((bf16[128,1024]{1,0:T(8,128)(2,1)S(1)}, bf16[128,1024]{1,0:T(8,128)(2,1)}, u32[]{:S(2)}) %copy-start.4) | copy-done | bytes 262168
  44.4 0.9 %copy-done.6 = bf16[128,1024]{1,0:T(8,128)(2,1)S(1)} copy-done((bf16[128,1024]{1,0:T(8,128)(2,1)S(1)}, bf16[128,1024]{1,0:T(8,128)(2,1)}, u32[]{:S(2)}) %copy-start.6) | copy-done | bytes 262168
  45.3 7.2 %precondition.3.refs_1_ = bf16[512,1024]{1,0:T(8,128)(2,1)} custom-call(s32[1]{0:T(128)} %bitcast.1.core, s32[13]{0:T(128)} %bitcast.22, s32[4]{0:T(128)} %bitcast.25, bf16[128,512]{1,0:T(8,128)(2,1)S(1)} %get-tuple-element.22.refs_0_, bf16[128,512]{1,0:T(8,128)(2,1)S(1)} %collective-permute-done.13.refs_1_, ...), custom_call_target="tpu_custom_call" | custom-call | flops 4563402752 | bytes 2097152 | tf_op jit(solution)/shard_map/precondition/pallas_call | solution.py:339
  52.5 0.7 collective-permute-start.2
  53.2 0.1 payload.3
  53.3 0.7 collective-permute-start.3
  54.0 0.1 payload.4
  54.1 1.3 %collective-permute-start.4 = (bf16[64,2048]{1,0:T(8,128)(2,1)S(1)}, bf16[64,2048]{1,0:T(8,128)(2,1)S(1)}, u32[]{:S(2)}, u32[]{:S(2)}) collective-permute-start(bf16[64,2048]{1,0:T(8,128)(2,1)S(1)} %payload.4), channel_id=1, source_target_pairs={{8,0},{16,8},{9,1},{17,9},{10,2},{18,10},{11,3},{19,11},{12,4},{20... | collective-permute-start | bytes 786440 | tf_op jit(solution)/shard_map/ppermute | solution.py:251
  55.4 13.9 %collective-permute-done.4.refs_0_.refs_3_ = bf16[64,2048]{1,0:T(8,128)(2,1)S(1)} collective-permute-done((bf16[64,2048]{1,0:T(8,128)(2,1)S(1)}, bf16[64,2048]{1,0:T(8,128)(2,1)S(1)}, u32[]{:S(2)}, u32[]{:S(2)}) %collective-permute-start.4) | collective-permute-done | bytes 262176 | tf_op jit(solution)/shard_map/ppermute | solution.py:251
  69.4 1.3 %collective-permute-start.5 = (bf16[64,2048]{1,0:T(8,128)(2,1)S(1)}, bf16[64,2048]{1,0:T(8,128)(2,1)S(1)}, u32[]{:S(2)}, u32[]{:S(2)}) collective-permute-start(bf16[64,2048]{1,0:T(8,128)(2,1)S(1)} %payload.5), channel_id=1, source_target_pairs={{8,0},{9,1},{10,2},{11,3},{12,4},{13,5},{14,6},{15,7}} | collective-permute-start | bytes 786440 | tf_op jit(solution)/shard_map/ppermute | solution.py:251
  70.7 10.5 %collective-permute-done.5.refs_4_ = bf16[64,2048]{1,0:T(8,128)(2,1)S(1)} collective-permute-done((bf16[64,2048]{1,0:T(8,128)(2,1)S(1)}, bf16[64,2048]{1,0:T(8,128)(2,1)S(1)}, u32[]{:S(2)}, u32[]{:S(2)}) %collective-permute-start.5) | collective-permute-done | bytes 262176 | tf_op jit(solution)/shard_map/ppermute | solution.py:251
  81.2 1.1 %finish.1 = bf16[128,2048]{1,0:T(8,128)(2,1)} custom-call(s32[1]{0:T(128)} %bitcast.section, bf16[128,2048]{1,0:T(8,128)(2,1)S(1)} %copy-done, bf16[128,2048]{1,0:T(8,128)(2,1)S(1)} %get-tuple-element.17.term.term_ref, bf16[64,2048]{1,0:T(8,128)(2,1)S(1)} %collective-permute-done.1.refs_0_, bf16[64,2048]{1,0:T(8,128)(2,1)S(1)} %collective-permute-done.2.refs_0_.refs_1_, ...), custom_call_target="tpu_custom_call" | custom-call | flops 524288 | bytes 2097152 | tf_op jit(solution)/shard_map/finish/pallas_call | solution.py:277
  82.3 3.6 %place_rows.1 = bf16[2048,1024]{1,0:T(8,128)(2,1)} custom-call(s32[1]{0:T(128)} %bitcast.1.core, bf16[512,1024]{1,0:T(8,128)(2,1)S(1)} %precondition.2.refs_0_, bf16[512,1024]{1,0:T(8,128)(2,1)} %precondition.3.refs_1_, bf16[512,1024]{1,0:T(8,128)(2,1)S(1)} %collective-permute-done.16.refs_2_, bf16[512,1024]{1,0:T(8,128)(2,1)} %collective-permute-done.17.refs_3_), custom_call_target="tpu_custom_call" | custom-call | bytes 8388608 | tf_op jit(solution)/shard_map/place_rows/pallas_call | solution.py:371
  (36 shorter events, 0.2 us)
Async XLA Ops:
  0.6 17.5 %copy-start.1 = (bf16[1,128,1024]{2,1,0:T(8,128)(2,1)S(1)}, bf16[1,128,1024]{2,1,0:T(8,128)(2,1)}, u32[]{:S(2)}) copy-start(bf16[1,128,1024]{2,1,0:T(8,128)(2,1)} %param.10) | copy-start | bytes 786436
  0.6 9.6 %collective-permute-start.10 = (bf16[128,1024]{1,0:T(8,128)(2,1)}, bf16[128,1024]{1,0:T(8,128)(2,1)S(1)}, u32[]{:S(2)}, u32[]{:S(2)}) collective-permute-start(bf16[128,1024]{1,0:T(8,128)(2,1)} %bitcast.10), channel_id=1, source_target_pairs={{0,4},{2,6},{4,0},{6,2},{1,5},{3,7},{5,1},{7,3},{8,12},{10,14},{12... | collective-permute-start | bytes 786440 | tf_op jit(solution)/shard_map/ppermute | solution.py:22
  3.7 14.4 %collective-permute-start.9 = (bf16[128,1024]{1,0:T(8,128)(2,1)}, bf16[128,1024]{1,0:T(8,128)(2,1)S(1)}, u32[]{:S(2)}, u32[]{:S(2)}) collective-permute-start(bf16[128,1024]{1,0:T(8,128)(2,1)} %bitcast.11), channel_id=1, source_target_pairs={{0,2},{2,0},{4,6},{6,4},{1,3},{3,1},{5,7},{7,5},{8,10},{10,8},{12,... | collective-permute-start | bytes 786440 | tf_op jit(solution)/shard_map/ppermute | solution.py:22
  10.2 24.3 %copy-start.3 = (bf16[128,1024]{1,0:T(8,128)(2,1)}, bf16[128,1024]{1,0:T(8,128)(2,1)S(1)}, u32[]{:S(2)}) copy-start(bf16[128,1024]{1,0:T(8,128)(2,1)S(1)} %collective-permute-done.10.refs_2_.refs_6_) | copy-start | bytes 786436
  10.2 7.9 %collective-permute-start.11 = (bf16[128,1024]{1,0:T(8,128)(2,1)S(1)}, bf16[128,1024]{1,0:T(8,128)(2,1)S(1)}, u32[]{:S(2)}, u32[]{:S(2)}) collective-permute-start(bf16[128,1024]{1,0:T(8,128)(2,1)S(1)} %collective-permute-done.10.refs_2_.refs_6_), channel_id=1, source_target_pairs={{0,2},{2,0},{4,6},{6,4},{1,3},{3,1},{5,7},{7,5},{8,10},{10,8},{12,... | collective-permute-start | bytes 786440 | tf_op jit(solution)/shard_map/ppermute | solution.py:22
  14.4 3.7 %collective-permute-start = (f32[8,128]{1,0:T(8,128)S(1)}, f32[8,128]{1,0:T(8,128)S(1)}, u32[]{:S(2)}, u32[]{:S(2)}) collective-permute-start(f32[8,128]{1,0:T(8,128)S(1)} %get-tuple-element.16.own_ref.own_stats), channel_id=1, source_target_pairs={{0,1},{1,0},{2,3},{3,2},{4,5},{5,4},{6,7},{7,6},{8,9},{9,8},{10,11... | collective-permute-start | bytes 12296 | tf_op jit(solution)/shard_map/ppermute | solution.py:22
  18.1 16.4 %copy-start.5 = (bf16[128,1024]{1,0:T(8,128)(2,1)}, bf16[128,1024]{1,0:T(8,128)(2,1)S(1)}, u32[]{:S(2)}) copy-start(bf16[128,1024]{1,0:T(8,128)(2,1)S(1)} %collective-permute-done.9.refs_1_.refs_5_) | copy-start | bytes 786436
  18.1 4.5 %copy-start.7 = (bf16[128,1024]{1,0:T(8,128)(2,1)}, bf16[128,1024]{1,0:T(8,128)(2,1)S(1)}, u32[]{:S(2)}) copy-start(bf16[128,1024]{1,0:T(8,128)(2,1)S(1)} %collective-permute-done.11.refs_3_.refs_7_) | copy-start | bytes 786436
  22.6 11.9 %collective-permute-start.12 = (bf16[512,512]{1,0:T(8,128)(2,1)S(1)}, bf16[512,512]{1,0:T(8,128)(2,1)S(1)}, u32[]{:S(2)}, u32[]{:S(2)}) collective-permute-start(bf16[512,512]{1,0:T(8,128)(2,1)S(1)} %value_inverse.1.refs_8_), channel_id=1, source_target_pairs={{0,2},{2,0},{4,6},{6,4},{1,3},{3,1},{5,7},{7,5},{8,10},{10,8},{12,... | collective-permute-start | bytes 1572872 | tf_op jit(solution)/shard_map/ppermute | solution.py:22
  23.7 10.0 %copy-start.10 = (bf16[64,2048]{1,0:T(8,128)(2,1)}, bf16[64,2048]{1,0:T(8,128)(2,1)S(1)}, u32[]{:S(2)}) copy-start(bf16[64,2048]{1,0:T(8,128)(2,1)S(1)} %get-tuple-element.19) | copy-start | bytes 786436
  23.7 6.4 %collective-permute-start.7 = (bf16[128,512]{1,0:T(8,128)(2,1)S(1)}, bf16[128,512]{1,0:T(8,128)(2,1)S(1)}, u32[]{:S(2)}, u32[]{:S(2)}) collective-permute-start(bf16[128,512]{1,0:T(8,128)(2,1)S(1)} %get-tuple-element.20.refs_0_), channel_id=1, source_target_pairs={{0,4},{2,6},{4,0},{6,2},{1,5},{3,7},{5,1},{7,3},{8,12},{10,14},{12... | collective-permute-start | bytes 393224 | tf_op jit(solution)/shard_map/ppermute | solution.py:22
  25.5 6.7 %collective-permute-start.8 = (bf16[128,512]{1,0:T(8,128)(2,1)S(1)}, bf16[128,512]{1,0:T(8,128)(2,1)S(1)}, u32[]{:S(2)}, u32[]{:S(2)}) collective-permute-start(bf16[128,512]{1,0:T(8,128)(2,1)S(1)} %get-tuple-element.21), channel_id=1, source_target_pairs={{0,6},{2,4},{4,2},{6,0},{1,7},{3,5},{5,3},{7,1},{8,14},{10,12},{12... | collective-permute-start | bytes 393224 | tf_op jit(solution)/shard_map/ppermute | solution.py:22
  25.6 8.1 %collective-permute-start.6 = (bf16[128,512]{1,0:T(8,128)(2,1)S(1)}, bf16[128,512]{1,0:T(8,128)(2,1)S(1)}, u32[]{:S(2)}, u32[]{:S(2)}) collective-permute-start(bf16[128,512]{1,0:T(8,128)(2,1)S(1)} %get-tuple-element.21), channel_id=1, source_target_pairs={{0,2},{2,0},{4,6},{6,4},{1,3},{3,1},{5,7},{7,5},{8,10},{10,8},{12,... | collective-permute-start | bytes 393224 | tf_op jit(solution)/shard_map/ppermute | solution.py:22
  25.9 17.6 %collective-permute-start.15 = (bf16[128,512]{1,0:T(8,128)(2,1)S(1)}, bf16[128,512]{1,0:T(8,128)(2,1)S(1)}, u32[]{:S(2)}, u32[]{:S(2)}) collective-permute-start(bf16[128,512]{1,0:T(8,128)(2,1)S(1)} %get-tuple-element.23), channel_id=1, source_target_pairs={{0,6},{2,4},{4,2},{6,0},{1,7},{3,5},{5,3},{7,1},{8,14},{10,12},{12... | collective-permute-start | bytes 393224 | tf_op jit(solution)/shard_map/ppermute | solution.py:22
  30.1 13.3 %collective-permute-start.13 = (bf16[128,512]{1,0:T(8,128)(2,1)S(1)}, bf16[128,512]{1,0:T(8,128)(2,1)S(1)}, u32[]{:S(2)}, u32[]{:S(2)}) collective-permute-start(bf16[128,512]{1,0:T(8,128)(2,1)S(1)} %get-tuple-element.23), channel_id=1, source_target_pairs={{0,2},{2,0},{4,6},{6,4},{1,3},{3,1},{5,7},{7,5},{8,10},{10,8},{12,... | collective-permute-start | bytes 393224 | tf_op jit(solution)/shard_map/ppermute | solution.py:22
  32.2 11.2 %collective-permute-start.14 = (bf16[128,512]{1,0:T(8,128)(2,1)S(1)}, bf16[128,512]{1,0:T(8,128)(2,1)S(1)}, u32[]{:S(2)}, u32[]{:S(2)}) collective-permute-start(bf16[128,512]{1,0:T(8,128)(2,1)S(1)} %get-tuple-element.22.refs_0_), channel_id=1, source_target_pairs={{0,4},{2,6},{4,0},{6,2},{1,5},{3,7},{5,1},{7,3},{8,12},{10,14},{12... | collective-permute-start | bytes 393224 | tf_op jit(solution)/shard_map/ppermute | solution.py:22
  33.7 9.7 %copy-start.2 = (bf16[1,128,1024]{2,1,0:T(8,128)(2,1)S(1)}, bf16[1,128,1024]{2,1,0:T(8,128)(2,1)}, u32[]{:S(2)}) copy-start(bf16[1,128,1024]{2,1,0:T(8,128)(2,1)} %param.10) | copy-start | bytes 786436
  33.7 19.5 %collective-permute-start.1 = (bf16[64,2048]{1,0:T(8,128)(2,1)}, bf16[64,2048]{1,0:T(8,128)(2,1)S(1)}, u32[]{:S(2)}, u32[]{:S(2)}) collective-permute-start(bf16[64,2048]{1,0:T(8,128)(2,1)} %get-tuple-element.18), channel_id=1, source_target_pairs={{24,16},{25,17},{26,18},{27,19},{28,20},{29,21},{30,22},{31,23}} | collective-permute-start | bytes 786440 | tf_op jit(solution)/shard_map/ppermute | solution.py:243
  34.5 1.0 %copy-start.8 = (bf16[128,1024]{1,0:T(8,128)(2,1)S(1)}, bf16[128,1024]{1,0:T(8,128)(2,1)}, u32[]{:S(2)}) copy-start(bf16[128,1024]{1,0:T(8,128)(2,1)} %copy-done.7) | copy-start | bytes 786436
  35.5 7.9 %copy-start.9 = (bf16[128,1024]{1,0:T(8,128)(2,1)S(1)}, bf16[128,1024]{1,0:T(8,128)(2,1)}, u32[]{:S(2)}) copy-start(bf16[128,1024]{1,0:T(8,128)(2,1)} %copy-done.7) | copy-start | bytes 786436
  40.4 40.8 %copy-start = (bf16[128,2048]{1,0:T(8,128)(2,1)S(1)}, bf16[128,2048]{1,0:T(8,128)(2,1)}, u32[]{:S(2)}) copy-start(bf16[128,2048]{1,0:T(8,128)(2,1)} %top_ref.1) | copy-start | bytes 1572868
  40.4 41.9 %collective-permute-start.16 = (bf16[512,1024]{1,0:T(8,128)(2,1)S(1)}, bf16[512,1024]{1,0:T(8,128)(2,1)S(1)}, u32[]{:S(2)}, u32[]{:S(2)}) collective-permute-start(bf16[512,1024]{1,0:T(8,128)(2,1)S(1)} %precondition.2.refs_0_), channel_id=1, source_target_pairs={{0,2},{2,0},{4,6},{6,4},{1,3},{3,1},{5,7},{7,5},{8,10},{10,8},{12,... | collective-permute-start | bytes 3145736 | tf_op jit(solution)/shard_map/ppermute | solution.py:22
  43.4 1.0 %copy-start.4 = (bf16[128,1024]{1,0:T(8,128)(2,1)S(1)}, bf16[128,1024]{1,0:T(8,128)(2,1)}, u32[]{:S(2)}) copy-start(bf16[128,1024]{1,0:T(8,128)(2,1)} %copy-done.3) | copy-start | bytes 786436
  44.4 0.9 %copy-start.6 = (bf16[128,1024]{1,0:T(8,128)(2,1)S(1)}, bf16[128,1024]{1,0:T(8,128)(2,1)}, u32[]{:S(2)}) copy-start(bf16[128,1024]{1,0:T(8,128)(2,1)} %copy-done.5) | copy-start | bytes 786436
  52.5 29.8 %collective-permute-start.17 = (bf16[512,1024]{1,0:T(8,128)(2,1)}, bf16[512,1024]{1,0:T(8,128)(2,1)}, u32[]{:S(2)}, u32[]{:S(2)}) collective-permute-start(bf16[512,1024]{1,0:T(8,128)(2,1)} %precondition.3.refs_1_), channel_id=1, source_target_pairs={{0,2},{2,0},{4,6},{6,4},{1,3},{3,1},{5,7},{7,5},{8,10},{10,8},{12,... | collective-permute-start | bytes 3145736 | tf_op jit(solution)/shard_map/ppermute | solution.py:22
  52.5 1.4 %collective-permute-start.2 = (bf16[64,2048]{1,0:T(8,128)(2,1)}, bf16[64,2048]{1,0:T(8,128)(2,1)S(1)}, u32[]{:S(2)}, u32[]{:S(2)}) collective-permute-start(bf16[64,2048]{1,0:T(8,128)(2,1)} %copy-done.10), channel_id=1, source_target_pairs={{24,16},{25,17},{26,18},{27,19},{28,20},{29,21},{30,22},{31,23}} | collective-permute-start | bytes 786440 | tf_op jit(solution)/shard_map/ppermute | solution.py:243
  53.3 0.7 collective-permute-start.3
  54.1 15.2 %collective-permute-start.4 = (bf16[64,2048]{1,0:T(8,128)(2,1)S(1)}, bf16[64,2048]{1,0:T(8,128)(2,1)S(1)}, u32[]{:S(2)}, u32[]{:S(2)}) collective-permute-start(bf16[64,2048]{1,0:T(8,128)(2,1)S(1)} %payload.4), channel_id=1, source_target_pairs={{8,0},{16,8},{9,1},{17,9},{10,2},{18,10},{11,3},{19,11},{12,4},{20... | collective-permute-start | bytes 786440 | tf_op jit(solution)/shard_map/ppermute | solution.py:251
  69.4 11.8 %collective-permute-start.5 = (bf16[64,2048]{1,0:T(8,128)(2,1)S(1)}, bf16[64,2048]{1,0:T(8,128)(2,1)S(1)}, u32[]{:S(2)}, u32[]{:S(2)}) collective-permute-start(bf16[64,2048]{1,0:T(8,128)(2,1)S(1)} %payload.5), channel_id=1, source_target_pairs={{8,0},{9,1},{10,2},{11,3},{12,4},{13,5},{14,6},{15,7}} | collective-permute-start | bytes 786440 | tf_op jit(solution)/shard_map/ppermute | solution.py:251
